TPU v7x, 256 devices: a whole 4x4x8 slice. The times are simulated.
256 devices in a mesh: gx: 64 (over y, z, core), gy: 4 (over x).
Axes of the slice: x: 4, y: 4, z: 8, core: 2. Of those that a mesh axis runs over, the one named last changes fastest.
Arguments:
- rhs: float32 [512, 256, 256], P('gx', 'gy'), may hold values from -12 to 12
- coefs: float32 [13, 512, 256, 256], P(None, 'gx', 'gy'), may hold values from 0 to 1.4, as said below
- shifts: float32 [4], replicated, may hold values from 0.4 to 1.1
Outputs:
- basis: float32 [5, 512, 256, 256], P(None, 'gx', 'gy')
- factor: float32 [5, 5], replicated
- solution: float32 [512, 256, 256], P('gx', 'gy')
- residual: float32 [512, 256, 256], P('gx', 'gy')
Inputs may be any that keep to these rules, and one draw needn't show every extreme that they name: `coefs`: entry 0 lies in 0.6 to 1.4, entries 1 to 6 in 0.02 to 0.22, entries 7 to 12 in 0 to 0.16.
All inputs are finite; a program needn't handle non-finite values.
Results may differ from a plain program's by a relative error of at most 0.00095.
Values sent between devices are 32-bit elements; how exact they have to be, the bound alone decides.
No kernel may reach another device: no remote copies, remote signals or barrier semaphores. Data moves between devices by JAX's collectives and lax.ppermute only.
A program may use at most 64 MiB of HBM per device.

v0:
```python
import jax
import jax.numpy as jnp
from jax import lax
from jax.experimental import pallas as pl
from jax.experimental.pallas import tpu as pltpu
from jax.sharding import Mesh
from jax.sharding import PartitionSpec as P

GX = ("gx_0", "gx_1", "gx_2")
EVERY = ("gx_0", "gx_1", "gx_2", "gy")
F32 = jnp.float32
GROWTH = 2.0
LIMIT = 48 * 1024 * 1024

VM = pl.BlockSpec(memory_space=pltpu.VMEM)
SM = pl.BlockSpec(memory_space=pltpu.SMEM)
ANY = pl.BlockSpec(memory_space=pl.ANY)


def on_chip(*shape):
    return pltpu.VMEM(shape, F32)


def pinned(array):
    return pltpu.with_memory_space_constraint(array, pltpu.VMEM)


def call(kernel, name, ins, specs, outs, out_specs=None, scratch=()):
    ins = [pinned(a) if s is VM else a for a, s in zip(ins, specs)]
    return pl.pallas_call(
        kernel,
        name=name,
        out_shape=outs,
        in_specs=specs,
        out_specs=out_specs if out_specs is not None else [VM] * len(outs),
        scratch_shapes=scratch,
        compiler_params=pltpu.CompilerParams(vmem_limit_bytes=LIMIT),
    )(*ins)


def shifted(plane, above, below):
    rows, lanes = plane.shape
    row = lax.broadcasted_iota(jnp.int32, plane.shape, 0)
    lane = lax.broadcasted_iota(jnp.int32, plane.shape, 1)
    minus_y = jnp.where(row == 0, above, pltpu.roll(plane, 1, 0))
    plus_y = jnp.where(row == rows - 1, below, pltpu.roll(plane, rows - 1, 0))
    minus_z = jnp.where(lane == 0, 0.0, pltpu.roll(plane, 1, 1))
    plus_z = jnp.where(lane == lanes - 1, 0.0, pltpu.roll(plane, lanes - 1, 1))
    return minus_y, plus_y, minus_z, plus_z


def neighbours(field, p, halo, edge):
    minus_x, plus_x, above, below = halo
    planes = field.shape[0]
    centre = field[p]
    before = minus_x[...] if p == 0 else field[p - 1]
    after = plus_x[...] if p == planes - 1 else field[p + 1]
    up = above[p : p + 1, :] * edge[0]
    down = below[p : p + 1, :] * edge[1]
    return centre, (before, after) + shifted(centre, up, down)


def put_edges(p, value, planes, x_low, x_high, y_low, y_high):
    rows = value.shape[0]
    if p == 0:
        x_low[...] = value
    if p == planes - 1:
        x_high[...] = value
    y_low[p : p + 1, :] = value[:1]
    y_high[p : p + 1, :] = value[rows - 1 :]


def load_kernel(coefs, wide, sems):
    copies = [pltpu.make_async_copy(coefs.at[i], wide.at[i], sems.at[i]) for i in range(coefs.shape[0])]
    for copy in copies:
        copy.start()
    for copy in copies:
        copy.wait()


def edge_kernel(rhs, x_low, x_high, y_low, y_high):
    planes = rhs.shape[0]
    for p in range(planes):
        put_edges(p, rhs[p], planes, x_low, x_high, y_low, y_high)


def spai_kernel(edge, coefs, v, mx, px, my, py, w, x_low, x_high, y_low, y_high):
    planes = v.shape[0]
    for p in range(planes):
        centre, near = neighbours(v, p, (mx, px, my, py), edge)
        total = coefs[0, p] * centre
        for d in range(6):
            total = total + coefs[1 + d, p] * near[d]
        w[p] = total
        put_edges(p, total, planes, x_low, x_high, y_low, y_high)


def apply_kernel(edge, coefs, shift, v, w, mx, px, my, py, out, x_low, x_high, y_low, y_high):
    planes = v.shape[0]
    for p in range(planes):
        centre, near = neighbours(w, p, (mx, px, my, py), edge)
        total = centre
        for d in range(6):
            total = total - coefs[7 + d, p] * near[d]
        total = GROWTH * (total - shift[0] * v[p])
        out[p] = total
        put_edges(p, total, planes, x_low, x_high, y_low, y_high)


def pair_rows(count):
    return [(i, j) for j in range(count) for i in range(j + 1)]


def gram_accumulate(lefts, right, rows):
    planes = right.shape[0]
    sums = [jnp.zeros((8, 256), F32) for _ in lefts]
    for p in range(planes):
        for r in range(0, right.shape[1], 8):
            value = right[p, r : r + 8, :]
            for k, left in enumerate(lefts):
                other = value if left is right else left[p, r : r + 8, :]
                sums[k] = sums[k] + other * value
    return [jnp.sum(s[:, :128] + s[:, 128:], axis=0, keepdims=True) for s in sums]


def early_gram_kernel(v0, v1, v2, v3, out):
    fields = (v0, v1, v2, v3)
    k = 0
    out[...] = jnp.zeros_like(out)
    for j in range(4):
        for part in gram_accumulate(fields[: j + 1], fields[j], None):
            out[k : k + 1, :] = part
            k += 1


def late_gram_kernel(early, v0, v1, v2, v3, v4, out, hold):
    fields = (v0, v1, v2, v3, v4)
    hold[...] = early[...]
    for k, part in enumerate(gram_accumulate(fields, v4, None)):
        hold[10 + k : 11 + k, :] = part
    totals = jnp.sum(hold[...], axis=1, keepdims=True)
    row = lax.broadcasted_iota(jnp.int32, (16, 128), 0)
    lane = lax.broadcasted_iota(jnp.int32, (16, 128), 1)
    line = jnp.sum(jnp.where(row == lane, totals, 0.0), axis=0, keepdims=True)
    out[...] = jnp.broadcast_to(line, out.shape)


def solve(gram, shifts):
    n = 5
    zero = jnp.zeros_like(gram[0][0])
    one = jnp.ones_like(zero)
    lower = [[zero] * n for _ in range(n)]
    for j in range(n):
        rest = gram[j][j]
        for k in range(j):
            rest = rest - lower[j][k] * lower[j][k]
        pivot = jnp.sqrt(rest)
        lower[j][j] = pivot
        for i in range(j + 1, n):
            rest = gram[i][j]
            for k in range(j):
                rest = rest - lower[i][k] * lower[j][k]
            lower[i][j] = rest / pivot
    factor = [[lower[j][i] for j in range(n)] for i in range(n)]

    def invert(upper, order):
        result = [[zero] * order for _ in range(order)]
        for row in range(order - 1, -1, -1):
            for column in range(row, order):
                known = one if column == row else zero
                for k in range(row + 1, column + 1):
                    known = known - upper[row][k] * result[k][column]
                result[row][column] = known / upper[row][row]
        return result

    inverse = invert(factor, n)
    count = n - 1
    hess = [[None] * count for _ in range(n)]
    for row in range(n):
        for column in range(count):
            entry = zero
            if column >= row:
                entry = entry + factor[row][column] * shifts[column]
            if column + 1 >= row:
                entry = entry + factor[row][column + 1] * (1.0 / GROWTH)
            hess[row][column] = entry
    target = [factor[0][0]] + [zero] * (n - 1)
    for column in range(count):
        top, below = hess[column], hess[column + 1]
        radius = jnp.sqrt(top[column] * top[column] + below[column] * below[column])
        cosine = top[column] / radius
        sine = below[column] / radius
        hess[column] = [cosine * t + sine * b for t, b in zip(top, below)]
        hess[column + 1] = [cosine * b - sine * t for t, b in zip(top, below)]
        first, second = target[column], target[column + 1]
        target[column] = cosine * first + sine * second
        target[column + 1] = cosine * second - sine * first
    upper_inverse = invert(hess, count)
    weights = []
    for row in range(count):
        entry = zero
        for k in range(row, count):
            entry = entry + upper_inverse[row][k] * target[k]
        weights.append(entry)
    combine = []
    for row in range(n):
        entry = one if row == 0 else zero
        if row < count:
            entry = entry - shifts[row] * weights[row]
        if row > 0:
            entry = entry - (1.0 / GROWTH) * weights[row - 1]
        combine.append(entry)
    return factor, inverse, weights, combine


def final_kernel(cells, shifts, rows, v0, v1, v2, v3, v4, w0, w1, w2, w3,
                 basis, factor_out, solution_out, residual_out, made, sems):
    line = jnp.sum(rows[...], axis=0, keepdims=True) * (1.0 / cells)
    gram = [[None] * 5 for _ in range(5)]
    for k, (i, j) in enumerate(pair_rows(5)):
        entry = jnp.broadcast_to(line[:, k : k + 1], (8, 128))
        gram[i][j] = entry
        gram[j][i] = entry
    factor, inverse, weights, combine = solve(gram, [shifts[k] for k in range(4)])
    row = lax.broadcasted_iota(jnp.int32, (8, 128), 0)
    lane = lax.broadcasted_iota(jnp.int32, (8, 128), 1)
    table = jnp.zeros((8, 128), F32)
    for i in range(5):
        for j in range(i, 5):
            table = jnp.where((row == i) & (lane == j), factor[i][j], table)
    factor_out[...] = table[:5, :5]
    fields = (v0, v1, v2, v3, v4)
    images = (w0, w1, w2, w3)
    planes = v0.shape[0]
    copies = []
    for p in range(planes):
        for r in range(0, v0.shape[1], 8):
            for c in range(0, v0.shape[2], 128):
                v = [f[p, r : r + 8, c : c + 128] for f in fields]
                w = [f[p, r : r + 8, c : c + 128] for f in images]
                for k in range(5):
                    total = inverse[0][k] * v[0]
                    for j in range(1, k + 1):
                        total = total + inverse[j][k] * v[j]
                    made[k, p, r : r + 8, c : c + 128] = total
                total = weights[0] * w[0]
                for k in range(1, 4):
                    total = total + weights[k] * w[k]
                made[5, p, r : r + 8, c : c + 128] = total
                total = combine[0] * v[0]
                for j in range(1, 5):
                    total = total + combine[j] * v[j]
                made[6, p, r : r + 8, c : c + 128] = total
        for n, (source, target) in enumerate(
            ((made.at[0:5, p], basis.at[:, p]), (made.at[5, p], solution_out.at[p]), (made.at[6, p], residual_out.at[p]))
        ):
            copy = pltpu.make_async_copy(source, target, sems.at[p, n])
            copy.start()
            copies.append(copy)
    for copy in copies:
        copy.wait()


def ring(count, step):
    return [(i, (i + step) % count) for i in range(count)]


def exchange(edges):
    x_low, x_high, y_low, y_high = edges
    nx, ny = lax.axis_size(GX), lax.axis_size("gy")
    return (
        lax.ppermute(x_high, GX, ring(nx, 1)),
        lax.ppermute(x_low, GX, ring(nx, -1)),
        lax.ppermute(y_high, "gy", ring(ny, 1)),
        lax.ppermute(y_low, "gy", ring(ny, -1)),
    )


def body(rhs, coefs, shifts):
    planes, rows, lanes = rhs.shape
    field = on_chip(planes, rows, lanes)
    edges = [on_chip(rows, lanes), on_chip(rows, lanes), on_chip(planes, lanes), on_chip(planes, lanes)]
    place = lax.axis_index("gy")
    last = lax.axis_size("gy") - 1
    edge = jnp.stack([(place > 0).astype(F32), (place < last).astype(F32)])
    (near,) = call(
        load_kernel, "load", [coefs], [ANY], [on_chip(*coefs.shape)],
        scratch=[pltpu.SemaphoreType.DMA((coefs.shape[0],))],
    )
    halo = exchange(call(edge_kernel, "edges", [rhs], [VM], edges))
    basis, images = [rhs], []
    for step in range(4):
        w, *cut = call(spai_kernel, "spai", [edge, near, basis[step], *halo], [SM] + [VM] * 6, [field] + edges)
        images.append(w)
        halo = exchange(cut)
        v, *cut = call(
            apply_kernel, "apply", [edge, near, shifts[step : step + 1], basis[step], w, *halo],
            [SM, VM, SM] + [VM] * 6, [field] + edges,
        )
        basis.append(v)
        if step < 3:
            halo = exchange(cut)
    (early,) = call(early_gram_kernel, "early_gram", basis[:4], [VM] * 4, [on_chip(16, 128)])
    devices = lax.axis_size(GX) * lax.axis_size("gy")
    (line,) = call(
        late_gram_kernel, "late_gram", [early, *basis], [VM] * 6, [on_chip(devices, 128)],
        scratch=[pltpu.VMEM((16, 128), F32)],
    )
    lines = lax.all_to_all(line, EVERY, 0, 0, tiled=True)
    cells = float(planes * rows * lanes * devices)
    whole = jax.ShapeDtypeStruct((planes, rows, lanes), F32)
    return tuple(
        call(
            lambda *refs: final_kernel(cells, *refs), "final",
            [shifts, lines, *basis, *images], [SM] + [VM] * 10,
            [jax.ShapeDtypeStruct((5, planes, rows, lanes), F32), jax.ShapeDtypeStruct((5, 5), F32), whole, whole],
            out_specs=[ANY, VM, ANY, ANY],
            scratch=[pltpu.VMEM((7, planes, rows, lanes), F32), pltpu.SemaphoreType.DMA((planes, 3))],
        )
    )


def solution(mesh):
    torus = Mesh(mesh.devices.reshape(4, 8, 2, mesh.shape["gy"]), EVERY)
    in_specs = (P(GX, "gy", None), P(None, GX, "gy", None), P())
    out_specs = (P(None, GX, "gy", None), P(), P(GX, "gy", None), P(GX, "gy", None))
    return jax.shard_map(body, mesh=torus, in_specs=in_specs, out_specs=out_specs, check_vma=False)
```

profile of v0, /device:TPU:1, one launch (start us, length us, event | category | flops | bytes accessed | tf_op | source)
XLA Modules:
  0.0 125.2 jit_solution(997260374337940571)
XLA Ops:
  0.6 1.0 copy-done
  1.7 3.1 %collective-permute-start = (f32[64,256]{1,0:T(8,128)S(1)}, f32[64,256]{1,0:T(8,128)S(1)}, u32[]{:S(2)}, u32[]{:S(2)}) collective-permute-start(f32[64,256]{1,0:T(8,128)S(1)} %get-tuple-element.44), channel_id=1, source_target_pairs={{0,4},{4,8},{8,12},{12,16},{16,20},{20,24},{24,28},{28,32},{32,36}... | collective-permute-start | bytes 196616 | tf_op jit(solution)/shard_map/ppermute | solution.py:272
  4.8 0.3 collective-permute-start.1
  5.1 0.9 collective-permute-start.2
  6.0 1.8 %collective-permute-start.3 = (f32[8,256]{1,0:T(8,128)S(1)}, f32[8,256]{1,0:T(8,128)S(1)}, u32[]{:S(2)}, u32[]{:S(2)}) collective-permute-start(f32[8,256]{1,0:T(8,128)S(1)} %get-tuple-element.47), channel_id=1, source_target_pairs={{0,3},{1,0},{2,1},{3,2},{4,7},{5,4},{6,5},{7,6},{8,11},{9,8},{10,9... | collective-permute-start | bytes 24584 | tf_op jit(solution)/shard_map/ppermute | solution.py:275
  7.8 0.6 add_convert_fusion.edge
  8.4 3.1 %load.1.coefs = f32[13,8,64,256]{3,2,1,0:T(8,128)S(1)} custom-call(f32[13,8,64,256]{3,2,1,0:T(8,128)} %coefs.1), custom_call_target="tpu_custom_call" | custom-call | tf_op jit(solution)/shard_map/load/pallas_call | solution.py:30
  11.6 1.1 spai.4
  12.7 2.1 %collective-permute-start.4 = (f32[64,256]{1,0:T(8,128)S(1)}, f32[64,256]{1,0:T(8,128)S(1)}, u32[]{:S(2)}, u32[]{:S(2)}) collective-permute-start(f32[64,256]{1,0:T(8,128)S(1)} %get-tuple-element.49), channel_id=1, source_target_pairs={{0,4},{4,8},{8,12},{12,16},{16,20},{20,24},{24,28},{28,32},{32,36}... | collective-permute-start | bytes 196616 | tf_op jit(solution)/shard_map/ppermute | solution.py:272
  14.8 4.7 %collective-permute-start.5 = (f32[64,256]{1,0:T(8,128)S(1)}, f32[64,256]{1,0:T(8,128)S(1)}, u32[]{:S(2)}, u32[]{:S(2)}) collective-permute-start(f32[64,256]{1,0:T(8,128)S(1)} %get-tuple-element.50), channel_id=1, source_target_pairs={{0,252},{4,0},{8,4},{12,8},{16,12},{20,16},{24,20},{28,24},{32,28}... | collective-permute-start | bytes 196616 | tf_op jit(solution)/shard_map/ppermute | solution.py:273
  19.5 2.7 %collective-permute-start.7 = (f32[8,256]{1,0:T(8,128)S(1)}, f32[8,256]{1,0:T(8,128)S(1)}, u32[]{:S(2)}, u32[]{:S(2)}) collective-permute-start(f32[8,256]{1,0:T(8,128)S(1)} %get-tuple-element.52), channel_id=1, source_target_pairs={{0,3},{1,0},{2,1},{3,2},{4,7},{5,4},{6,5},{7,6},{8,11},{9,8},{10,9... | collective-permute-start | bytes 24584 | tf_op jit(solution)/shard_map/ppermute | solution.py:275
  22.2 0.6 fusion
  22.8 0.4 collective-permute-done.6.my
  23.2 1.8 %apply.4 = (f32[8,64,256]{2,1,0:T(8,128)S(1)}, f32[64,256]{1,0:T(8,128)S(1)}, f32[64,256]{1,0:T(8,128)S(1)}, f32[8,256]{1,0:T(8,128)S(1)}, f32[8,256]{1,0:T(8,128)S(1)}) custom-call(f32[2]{0:T(128)} %add_convert_fusion.edge, f32[13,8,64,256]{3,2,1,0:T(8,128)S(1)} %load.1.coefs, f32[1]{0:T(128)} %get-tuple-element.87.shift, f32[8,64,256]{2,1,0:T(8,128)S(1)} %copy-done.1, ...), custom_call_target="tpu_custom_call" | custom-call | tf_op jit(solution)/shard_map/apply/pallas_call | solution.py:30
  25.1 6.2 %collective-permute-start.9 = (f32[64,256]{1,0:T(8,128)S(1)}, f32[64,256]{1,0:T(8,128)S(1)}, u32[]{:S(2)}, u32[]{:S(2)}) collective-permute-start(f32[64,256]{1,0:T(8,128)S(1)} %get-tuple-element.55), channel_id=1, source_target_pairs={{0,252},{4,0},{8,4},{12,8},{16,12},{20,16},{24,20},{28,24},{32,28}... | collective-permute-start | bytes 196616 | tf_op jit(solution)/shard_map/ppermute | solution.py:273
  31.6 2.7 %collective-permute-start.11 = (f32[8,256]{1,0:T(8,128)S(1)}, f32[8,256]{1,0:T(8,128)S(1)}, u32[]{:S(2)}, u32[]{:S(2)}) collective-permute-start(f32[8,256]{1,0:T(8,128)S(1)} %get-tuple-element.57), channel_id=1, source_target_pairs={{0,3},{1,0},{2,1},{3,2},{4,7},{5,4},{6,5},{7,6},{8,11},{9,8},{10,9... | collective-permute-start | bytes 24584 | tf_op jit(solution)/shard_map/ppermute | solution.py:275
  34.3 1.0 collective-permute-done.10.my
  35.3 1.1 spai.5
  36.5 6.1 %collective-permute-start.13 = (f32[64,256]{1,0:T(8,128)S(1)}, f32[64,256]{1,0:T(8,128)S(1)}, u32[]{:S(2)}, u32[]{:S(2)}) collective-permute-start(f32[64,256]{1,0:T(8,128)S(1)} %get-tuple-element.60), channel_id=1, source_target_pairs={{0,252},{4,0},{8,4},{12,8},{16,12},{20,16},{24,20},{28,24},{32,28}... | collective-permute-start | bytes 196616 | tf_op jit(solution)/shard_map/ppermute | solution.py:273
  42.6 1.1 collective-permute-start.14
  43.8 1.8 %collective-permute-start.15 = (f32[8,256]{1,0:T(8,128)S(1)}, f32[8,256]{1,0:T(8,128)S(1)}, u32[]{:S(2)}, u32[]{:S(2)}) collective-permute-start(f32[8,256]{1,0:T(8,128)S(1)} %get-tuple-element.62), channel_id=1, source_target_pairs={{0,3},{1,0},{2,1},{3,2},{4,7},{5,4},{6,5},{7,6},{8,11},{9,8},{10,9... | collective-permute-start | bytes 24584 | tf_op jit(solution)/shard_map/ppermute | solution.py:275
  45.6 1.0 collective-permute-done.14.my
  46.6 1.8 %apply.5 = (f32[8,64,256]{2,1,0:T(8,128)S(1)}, f32[64,256]{1,0:T(8,128)S(1)}, f32[64,256]{1,0:T(8,128)S(1)}, f32[8,256]{1,0:T(8,128)S(1)}, f32[8,256]{1,0:T(8,128)S(1)}) custom-call(f32[2]{0:T(128)} %add_convert_fusion.edge, f32[13,8,64,256]{3,2,1,0:T(8,128)S(1)} %load.1.coefs, f32[1]{0:T(128)} %get-tuple-element.86.shift, ...), custom_call_target="tpu_custom_call" | custom-call | tf_op jit(solution)/shard_map/apply/pallas_call | solution.py:30
  48.5 5.9 %collective-permute-start.17 = (f32[64,256]{1,0:T(8,128)S(1)}, f32[64,256]{1,0:T(8,128)S(1)}, u32[]{:S(2)}, u32[]{:S(2)}) collective-permute-start(f32[64,256]{1,0:T(8,128)S(1)} %get-tuple-element.65), channel_id=1, source_target_pairs={{0,252},{4,0},{8,4},{12,8},{16,12},{20,16},{24,20},{28,24},{32,28}... | collective-permute-start | bytes 196616 | tf_op jit(solution)/shard_map/ppermute | solution.py:273
  54.5 1.7 %collective-permute-start.18 = (f32[8,256]{1,0:T(8,128)S(1)}, f32[8,256]{1,0:T(8,128)S(1)}, u32[]{:S(2)}, u32[]{:S(2)}) collective-permute-start(f32[8,256]{1,0:T(8,128)S(1)} %get-tuple-element.66), channel_id=1, source_target_pairs={{0,1},{1,2},{2,3},{3,0},{4,5},{5,6},{6,7},{7,4},{8,9},{9,10},{10,1... | collective-permute-start | bytes 24584 | tf_op jit(solution)/shard_map/ppermute | solution.py:274
  56.2 1.0 collective-permute-start.19
  57.2 1.0 collective-permute-done.18.my
  58.3 0.5 collective-permute-done.19.py
  58.7 1.1 spai.6
  60.0 6.5 %collective-permute-start.21 = (f32[64,256]{1,0:T(8,128)S(1)}, f32[64,256]{1,0:T(8,128)S(1)}, u32[]{:S(2)}, u32[]{:S(2)}) collective-permute-start(f32[64,256]{1,0:T(8,128)S(1)} %get-tuple-element.70), channel_id=1, source_target_pairs={{0,252},{4,0},{8,4},{12,8},{16,12},{20,16},{24,20},{28,24},{32,28}... | collective-permute-start | bytes 196616 | tf_op jit(solution)/shard_map/ppermute | solution.py:273
  66.4 0.9 collective-permute-start.22
  67.4 1.7 %collective-permute-start.23 = (f32[8,256]{1,0:T(8,128)S(1)}, f32[8,256]{1,0:T(8,128)S(1)}, u32[]{:S(2)}, u32[]{:S(2)}) collective-permute-start(f32[8,256]{1,0:T(8,128)S(1)} %get-tuple-element.72), channel_id=1, source_target_pairs={{0,3},{1,0},{2,1},{3,2},{4,7},{5,4},{6,5},{7,6},{8,11},{9,8},{10,9... | collective-permute-start | bytes 24584 | tf_op jit(solution)/shard_map/ppermute | solution.py:275
  69.1 1.0 collective-permute-done.22.my
  70.2 1.8 %apply.6 = (f32[8,64,256]{2,1,0:T(8,128)S(1)}, f32[64,256]{1,0:T(8,128)S(1)}, f32[64,256]{1,0:T(8,128)S(1)}, f32[8,256]{1,0:T(8,128)S(1)}, f32[8,256]{1,0:T(8,128)S(1)}) custom-call(f32[2]{0:T(128)} %add_convert_fusion.edge, f32[13,8,64,256]{3,2,1,0:T(8,128)S(1)} %load.1.coefs, f32[1]{0:T(128)} %get-tuple-element.85.shift, ...), custom_call_target="tpu_custom_call" | custom-call | tf_op jit(solution)/shard_map/apply/pallas_call | solution.py:30
  72.1 6.2 %collective-permute-start.25 = (f32[64,256]{1,0:T(8,128)S(1)}, f32[64,256]{1,0:T(8,128)S(1)}, u32[]{:S(2)}, u32[]{:S(2)}) collective-permute-start(f32[64,256]{1,0:T(8,128)S(1)} %get-tuple-element.75), channel_id=1, source_target_pairs={{0,252},{4,0},{8,4},{12,8},{16,12},{20,16},{24,20},{28,24},{32,28}... | collective-permute-start | bytes 196616 | tf_op jit(solution)/shard_map/ppermute | solution.py:273
  78.3 0.9 collective-permute-start.26
  79.2 2.0 %collective-permute-start.27 = (f32[8,256]{1,0:T(8,128)S(1)}, f32[8,256]{1,0:T(8,128)S(1)}, u32[]{:S(2)}, u32[]{:S(2)}) collective-permute-start(f32[8,256]{1,0:T(8,128)S(1)} %get-tuple-element.77), channel_id=1, source_target_pairs={{0,3},{1,0},{2,1},{3,2},{4,7},{5,4},{6,5},{7,6},{8,11},{9,8},{10,9... | collective-permute-start | bytes 24584 | tf_op jit(solution)/shard_map/ppermute | solution.py:275
  81.3 1.0 collective-permute-done.26.my
  82.3 1.1 spai.7
  83.5 5.9 %collective-permute-start.29 = (f32[64,256]{1,0:T(8,128)S(1)}, f32[64,256]{1,0:T(8,128)S(1)}, u32[]{:S(2)}, u32[]{:S(2)}) collective-permute-start(f32[64,256]{1,0:T(8,128)S(1)} %get-tuple-element.80), channel_id=1, source_target_pairs={{0,252},{4,0},{8,4},{12,8},{16,12},{20,16},{24,20},{28,24},{32,28}... | collective-permute-start | bytes 196616 | tf_op jit(solution)/shard_map/ppermute | solution.py:273
  89.4 1.1 collective-permute-start.30
  90.5 1.8 %collective-permute-start.31 = (f32[8,256]{1,0:T(8,128)S(1)}, f32[8,256]{1,0:T(8,128)S(1)}, u32[]{:S(2)}, u32[]{:S(2)}) collective-permute-start(f32[8,256]{1,0:T(8,128)S(1)} %get-tuple-element.82), channel_id=1, source_target_pairs={{0,3},{1,0},{2,1},{3,2},{4,7},{5,4},{6,5},{7,6},{8,11},{9,8},{10,9... | collective-permute-start | bytes 24584 | tf_op jit(solution)/shard_map/ppermute | solution.py:275
  92.4 0.5 early_gram.1.early
  92.9 0.5 collective-permute-done.30.my
  93.4 2.5 %apply.7 = (f32[8,64,256]{2,1,0:T(8,128)S(1)}, f32[64,256]{1,0:T(8,128)}, f32[64,256]{1,0:T(8,128)}, f32[8,256]{1,0:T(8,128)}, f32[8,256]{1,0:T(8,128)}) custom-call(f32[2]{0:T(128)} %add_convert_fusion.edge, f32[13,8,64,256]{3,2,1,0:T(8,128)S(1)} %load.1.coefs, f32[1]{0:T(128)} %get-tuple-element.84.shift, ...), custom_call_target="tpu_custom_call" | custom-call | tf_op jit(solution)/shard_map/apply/pallas_call | solution.py:30
  95.9 0.3 late_gram.1
  96.2 25.3 %all_to_all.11 = f32[256,1,128]{2,1,0:T(1,128)S(1)} all-to-all(f32[256,1,128]{2,1,0:T(1,128)S(1)} %bitcast.7), channel_id=1, replica_groups=mesh['gx_0'=4,'gx_1'=8,'gx_2'=2,'gy'=4] {'gx_0','gx_1','gx_2','gy'}, dimensions={0} | all-to-all | bytes 262144 | tf_op jit(solution)/shard_map/all_to_all | solution.py:309
  121.5 3.4 %final.1 = (f32[5,8,64,256]{3,2,1,0:T(8,128)}, f32[5,5]{1,0:T(8,128)}, f32[8,64,256]{2,1,0:T(8,128)}, f32[8,64,256]{2,1,0:T(8,128)}) custom-call(f32[4]{0:T(128)S(1)} %copy-done.2, f32[256,128]{1,0:T(8,128)S(1)} %bitcast.6, f32[8,64,256]{2,1,0:T(8,128)S(1)} %copy-done.1, f32[8,64,256]{2,1,0:T(8,128)S(1)} %get-tuple-element.53.v.v1.refs_3_, ...), custom_call_target="tpu_custom_call" | custom-call | tf_op jit(solution)/shard_map/final/pallas_call | solution.py:30
  (38 shorter events, 0.9 us)
Async XLA Ops:
  0.6 1.0 copy-start
  1.7 9.9 %collective-permute-start = (f32[64,256]{1,0:T(8,128)S(1)}, f32[64,256]{1,0:T(8,128)S(1)}, u32[]{:S(2)}, u32[]{:S(2)}) collective-permute-start(f32[64,256]{1,0:T(8,128)S(1)} %get-tuple-element.44), channel_id=1, source_target_pairs={{0,4},{4,8},{8,12},{12,16},{16,20},{20,24},{24,28},{28,32},{32,36}... | collective-permute-start | bytes 196616 | tf_op jit(solution)/shard_map/ppermute | solution.py:272
  4.8 6.8 %collective-permute-start.1 = (f32[64,256]{1,0:T(8,128)S(1)}, f32[64,256]{1,0:T(8,128)S(1)}, u32[]{:S(2)}, u32[]{:S(2)}) collective-permute-start(f32[64,256]{1,0:T(8,128)S(1)} %get-tuple-element.45), channel_id=1, source_target_pairs={{0,252},{4,0},{8,4},{12,8},{16,12},{20,16},{24,20},{28,24},{32,28}... | collective-permute-start | bytes 196616 | tf_op jit(solution)/shard_map/ppermute | solution.py:273
  5.1 6.4 %collective-permute-start.2 = (f32[8,256]{1,0:T(8,128)S(1)}, f32[8,256]{1,0:T(8,128)S(1)}, u32[]{:S(2)}, u32[]{:S(2)}) collective-permute-start(f32[8,256]{1,0:T(8,128)S(1)} %get-tuple-element.46), channel_id=1, source_target_pairs={{0,1},{1,2},{2,3},{3,0},{4,5},{5,6},{6,7},{7,4},{8,9},{9,10},{10,1... | collective-permute-start | bytes 24584 | tf_op jit(solution)/shard_map/ppermute | solution.py:274
  6.0 5.5 %collective-permute-start.3 = (f32[8,256]{1,0:T(8,128)S(1)}, f32[8,256]{1,0:T(8,128)S(1)}, u32[]{:S(2)}, u32[]{:S(2)}) collective-permute-start(f32[8,256]{1,0:T(8,128)S(1)} %get-tuple-element.47), channel_id=1, source_target_pairs={{0,3},{1,0},{2,1},{3,2},{4,7},{5,4},{6,5},{7,6},{8,11},{9,8},{10,9... | collective-permute-start | bytes 24584 | tf_op jit(solution)/shard_map/ppermute | solution.py:275
  8.4 3.2 %copy-start.1 = (f32[8,64,256]{2,1,0:T(8,128)S(1)}, f32[8,64,256]{2,1,0:T(8,128)}, u32[]{:S(2)}) copy-start(f32[8,64,256]{2,1,0:T(8,128)} %refs_2_.1) | copy-start | bytes 1572868
  11.5 10.6 %copy-start.2 = (f32[4]{0:T(128)S(1)}, f32[4]{0:T(128)}, u32[]{:S(2)}) copy-start(f32[4]{0:T(128)} %refs_0_.1) | copy-start | bytes 52
  12.7 10.5 %collective-permute-start.4 = (f32[64,256]{1,0:T(8,128)S(1)}, f32[64,256]{1,0:T(8,128)S(1)}, u32[]{:S(2)}, u32[]{:S(2)}) collective-permute-start(f32[64,256]{1,0:T(8,128)S(1)} %get-tuple-element.49), channel_id=1, source_target_pairs={{0,4},{4,8},{8,12},{12,16},{16,20},{20,24},{24,28},{28,32},{32,36}... | collective-permute-start | bytes 196616 | tf_op jit(solution)/shard_map/ppermute | solution.py:272
  14.8 8.4 %collective-permute-start.5 = (f32[64,256]{1,0:T(8,128)S(1)}, f32[64,256]{1,0:T(8,128)S(1)}, u32[]{:S(2)}, u32[]{:S(2)}) collective-permute-start(f32[64,256]{1,0:T(8,128)S(1)} %get-tuple-element.50), channel_id=1, source_target_pairs={{0,252},{4,0},{8,4},{12,8},{16,12},{20,16},{24,20},{28,24},{32,28}... | collective-permute-start | bytes 196616 | tf_op jit(solution)/shard_map/ppermute | solution.py:273
  19.5 3.7 %collective-permute-start.6 = (f32[8,256]{1,0:T(8,128)S(1)}, f32[8,256]{1,0:T(8,128)S(1)}, u32[]{:S(2)}, u32[]{:S(2)}) collective-permute-start(f32[8,256]{1,0:T(8,128)S(1)} %get-tuple-element.51), channel_id=1, source_target_pairs={{0,1},{1,2},{2,3},{3,0},{4,5},{5,6},{6,7},{7,4},{8,9},{9,10},{10,1... | collective-permute-start | bytes 24584 | tf_op jit(solution)/shard_map/ppermute | solution.py:274
  19.5 3.7 %collective-permute-start.7 = (f32[8,256]{1,0:T(8,128)S(1)}, f32[8,256]{1,0:T(8,128)S(1)}, u32[]{:S(2)}, u32[]{:S(2)}) collective-permute-start(f32[8,256]{1,0:T(8,128)S(1)} %get-tuple-element.52), channel_id=1, source_target_pairs={{0,3},{1,0},{2,1},{3,2},{4,7},{5,4},{6,5},{7,6},{8,11},{9,8},{10,9... | collective-permute-start | bytes 24584 | tf_op jit(solution)/shard_map/ppermute | solution.py:275
  25.0 10.3 %collective-permute-start.8 = (f32[64,256]{1,0:T(8,128)S(1)}, f32[64,256]{1,0:T(8,128)S(1)}, u32[]{:S(2)}, u32[]{:S(2)}) collective-permute-start(f32[64,256]{1,0:T(8,128)S(1)} %get-tuple-element.54), channel_id=1, source_target_pairs={{0,4},{4,8},{8,12},{12,16},{16,20},{20,24},{24,28},{28,32},{32,36}... | collective-permute-start | bytes 196616 | tf_op jit(solution)/shard_map/ppermute | solution.py:272
  25.1 10.2 %collective-permute-start.9 = (f32[64,256]{1,0:T(8,128)S(1)}, f32[64,256]{1,0:T(8,128)S(1)}, u32[]{:S(2)}, u32[]{:S(2)}) collective-permute-start(f32[64,256]{1,0:T(8,128)S(1)} %get-tuple-element.55), channel_id=1, source_target_pairs={{0,252},{4,0},{8,4},{12,8},{16,12},{20,16},{24,20},{28,24},{32,28}... | collective-permute-start | bytes 196616 | tf_op jit(solution)/shard_map/ppermute | solution.py:273
  31.3 4.0 %collective-permute-start.10 = (f32[8,256]{1,0:T(8,128)S(1)}, f32[8,256]{1,0:T(8,128)S(1)}, u32[]{:S(2)}, u32[]{:S(2)}) collective-permute-start(f32[8,256]{1,0:T(8,128)S(1)} %get-tuple-element.56), channel_id=1, source_target_pairs={{0,1},{1,2},{2,3},{3,0},{4,5},{5,6},{6,7},{7,4},{8,9},{9,10},{10,1... | collective-permute-start | bytes 24584 | tf_op jit(solution)/shard_map/ppermute | solution.py:274
  31.6 3.7 %collective-permute-start.11 = (f32[8,256]{1,0:T(8,128)S(1)}, f32[8,256]{1,0:T(8,128)S(1)}, u32[]{:S(2)}, u32[]{:S(2)}) collective-permute-start(f32[8,256]{1,0:T(8,128)S(1)} %get-tuple-element.57), channel_id=1, source_target_pairs={{0,3},{1,0},{2,1},{3,2},{4,7},{5,4},{6,5},{7,6},{8,11},{9,8},{10,9... | collective-permute-start | bytes 24584 | tf_op jit(solution)/shard_map/ppermute | solution.py:275
  36.4 10.2 %collective-permute-start.12 = (f32[64,256]{1,0:T(8,128)S(1)}, f32[64,256]{1,0:T(8,128)S(1)}, u32[]{:S(2)}, u32[]{:S(2)}) collective-permute-start(f32[64,256]{1,0:T(8,128)S(1)} %get-tuple-element.59), channel_id=1, source_target_pairs={{0,4},{4,8},{8,12},{12,16},{16,20},{20,24},{24,28},{28,32},{32,36}... | collective-permute-start | bytes 196616 | tf_op jit(solution)/shard_map/ppermute | solution.py:272
  36.5 10.1 %collective-permute-start.13 = (f32[64,256]{1,0:T(8,128)S(1)}, f32[64,256]{1,0:T(8,128)S(1)}, u32[]{:S(2)}, u32[]{:S(2)}) collective-permute-start(f32[64,256]{1,0:T(8,128)S(1)} %get-tuple-element.60), channel_id=1, source_target_pairs={{0,252},{4,0},{8,4},{12,8},{16,12},{20,16},{24,20},{28,24},{32,28}... | collective-permute-start | bytes 196616 | tf_op jit(solution)/shard_map/ppermute | solution.py:273
  42.6 4.0 %collective-permute-start.14 = (f32[8,256]{1,0:T(8,128)S(1)}, f32[8,256]{1,0:T(8,128)S(1)}, u32[]{:S(2)}, u32[]{:S(2)}) collective-permute-start(f32[8,256]{1,0:T(8,128)S(1)} %get-tuple-element.61), channel_id=1, source_target_pairs={{0,1},{1,2},{2,3},{3,0},{4,5},{5,6},{6,7},{7,4},{8,9},{9,10},{10,1... | collective-permute-start | bytes 24584 | tf_op jit(solution)/shard_map/ppermute | solution.py:274
  43.8 2.9 %collective-permute-start.15 = (f32[8,256]{1,0:T(8,128)S(1)}, f32[8,256]{1,0:T(8,128)S(1)}, u32[]{:S(2)}, u32[]{:S(2)}) collective-permute-start(f32[8,256]{1,0:T(8,128)S(1)} %get-tuple-element.62), channel_id=1, source_target_pairs={{0,3},{1,0},{2,1},{3,2},{4,7},{5,4},{6,5},{7,6},{8,11},{9,8},{10,9... | collective-permute-start | bytes 24584 | tf_op jit(solution)/shard_map/ppermute | solution.py:275
  48.4 10.3 %collective-permute-start.16 = (f32[64,256]{1,0:T(8,128)S(1)}, f32[64,256]{1,0:T(8,128)S(1)}, u32[]{:S(2)}, u32[]{:S(2)}) collective-permute-start(f32[64,256]{1,0:T(8,128)S(1)} %get-tuple-element.64), channel_id=1, source_target_pairs={{0,4},{4,8},{8,12},{12,16},{16,20},{20,24},{24,28},{28,32},{32,36}... | collective-permute-start | bytes 196616 | tf_op jit(solution)/shard_map/ppermute | solution.py:272
  48.5 10.2 %collective-permute-start.17 = (f32[64,256]{1,0:T(8,128)S(1)}, f32[64,256]{1,0:T(8,128)S(1)}, u32[]{:S(2)}, u32[]{:S(2)}) collective-permute-start(f32[64,256]{1,0:T(8,128)S(1)} %get-tuple-element.65), channel_id=1, source_target_pairs={{0,252},{4,0},{8,4},{12,8},{16,12},{20,16},{24,20},{28,24},{32,28}... | collective-permute-start | bytes 196616 | tf_op jit(solution)/shard_map/ppermute | solution.py:273
  54.5 3.8 %collective-permute-start.18 = (f32[8,256]{1,0:T(8,128)S(1)}, f32[8,256]{1,0:T(8,128)S(1)}, u32[]{:S(2)}, u32[]{:S(2)}) collective-permute-start(f32[8,256]{1,0:T(8,128)S(1)} %get-tuple-element.66), channel_id=1, source_target_pairs={{0,1},{1,2},{2,3},{3,0},{4,5},{5,6},{6,7},{7,4},{8,9},{9,10},{10,1... | collective-permute-start | bytes 24584 | tf_op jit(solution)/shard_map/ppermute | solution.py:274
  56.2 2.5 %collective-permute-start.19 = (f32[8,256]{1,0:T(8,128)S(1)}, f32[8,256]{1,0:T(8,128)S(1)}, u32[]{:S(2)}, u32[]{:S(2)}) collective-permute-start(f32[8,256]{1,0:T(8,128)S(1)} %get-tuple-element.67), channel_id=1, source_target_pairs={{0,3},{1,0},{2,1},{3,2},{4,7},{5,4},{6,5},{7,6},{8,11},{9,8},{10,9... | collective-permute-start | bytes 24584 | tf_op jit(solution)/shard_map/ppermute | solution.py:275
  59.9 10.3 %collective-permute-start.20 = (f32[64,256]{1,0:T(8,128)S(1)}, f32[64,256]{1,0:T(8,128)S(1)}, u32[]{:S(2)}, u32[]{:S(2)}) collective-permute-start(f32[64,256]{1,0:T(8,128)S(1)} %get-tuple-element.69), channel_id=1, source_target_pairs={{0,4},{4,8},{8,12},{12,16},{16,20},{20,24},{24,28},{28,32},{32,36}... | collective-permute-start | bytes 196616 | tf_op jit(solution)/shard_map/ppermute | solution.py:272
  60.0 10.2 %collective-permute-start.21 = (f32[64,256]{1,0:T(8,128)S(1)}, f32[64,256]{1,0:T(8,128)S(1)}, u32[]{:S(2)}, u32[]{:S(2)}) collective-permute-start(f32[64,256]{1,0:T(8,128)S(1)} %get-tuple-element.70), channel_id=1, source_target_pairs={{0,252},{4,0},{8,4},{12,8},{16,12},{20,16},{24,20},{28,24},{32,28}... | collective-permute-start | bytes 196616 | tf_op jit(solution)/shard_map/ppermute | solution.py:273
  66.4 3.7 %collective-permute-start.22 = (f32[8,256]{1,0:T(8,128)S(1)}, f32[8,256]{1,0:T(8,128)S(1)}, u32[]{:S(2)}, u32[]{:S(2)}) collective-permute-start(f32[8,256]{1,0:T(8,128)S(1)} %get-tuple-element.71), channel_id=1, source_target_pairs={{0,1},{1,2},{2,3},{3,0},{4,5},{5,6},{6,7},{7,4},{8,9},{9,10},{10,1... | collective-permute-start | bytes 24584 | tf_op jit(solution)/shard_map/ppermute | solution.py:274
  67.4 2.8 %collective-permute-start.23 = (f32[8,256]{1,0:T(8,128)S(1)}, f32[8,256]{1,0:T(8,128)S(1)}, u32[]{:S(2)}, u32[]{:S(2)}) collective-permute-start(f32[8,256]{1,0:T(8,128)S(1)} %get-tuple-element.72), channel_id=1, source_target_pairs={{0,3},{1,0},{2,1},{3,2},{4,7},{5,4},{6,5},{7,6},{8,11},{9,8},{10,9... | collective-permute-start | bytes 24584 | tf_op jit(solution)/shard_map/ppermute | solution.py:275
  72.0 10.3 %collective-permute-start.24 = (f32[64,256]{1,0:T(8,128)S(1)}, f32[64,256]{1,0:T(8,128)S(1)}, u32[]{:S(2)}, u32[]{:S(2)}) collective-permute-start(f32[64,256]{1,0:T(8,128)S(1)} %get-tuple-element.74), channel_id=1, source_target_pairs={{0,4},{4,8},{8,12},{12,16},{16,20},{20,24},{24,28},{28,32},{32,36}... | collective-permute-start | bytes 196616 | tf_op jit(solution)/shard_map/ppermute | solution.py:272
  72.1 10.2 %collective-permute-start.25 = (f32[64,256]{1,0:T(8,128)S(1)}, f32[64,256]{1,0:T(8,128)S(1)}, u32[]{:S(2)}, u32[]{:S(2)}) collective-permute-start(f32[64,256]{1,0:T(8,128)S(1)} %get-tuple-element.75), channel_id=1, source_target_pairs={{0,252},{4,0},{8,4},{12,8},{16,12},{20,16},{24,20},{28,24},{32,28}... | collective-permute-start | bytes 196616 | tf_op jit(solution)/shard_map/ppermute | solution.py:273
  78.3 4.0 %collective-permute-start.26 = (f32[8,256]{1,0:T(8,128)S(1)}, f32[8,256]{1,0:T(8,128)S(1)}, u32[]{:S(2)}, u32[]{:S(2)}) collective-permute-start(f32[8,256]{1,0:T(8,128)S(1)} %get-tuple-element.76), channel_id=1, source_target_pairs={{0,1},{1,2},{2,3},{3,0},{4,5},{5,6},{6,7},{7,4},{8,9},{9,10},{10,1... | collective-permute-start | bytes 24584 | tf_op jit(solution)/shard_map/ppermute | solution.py:274
  79.2 3.1 %collective-permute-start.27 = (f32[8,256]{1,0:T(8,128)S(1)}, f32[8,256]{1,0:T(8,128)S(1)}, u32[]{:S(2)}, u32[]{:S(2)}) collective-permute-start(f32[8,256]{1,0:T(8,128)S(1)} %get-tuple-element.77), channel_id=1, source_target_pairs={{0,3},{1,0},{2,1},{3,2},{4,7},{5,4},{6,5},{7,6},{8,11},{9,8},{10,9... | collective-permute-start | bytes 24584 | tf_op jit(solution)/shard_map/ppermute | solution.py:275
  83.4 10.0 %collective-permute-start.28 = (f32[64,256]{1,0:T(8,128)S(1)}, f32[64,256]{1,0:T(8,128)S(1)}, u32[]{:S(2)}, u32[]{:S(2)}) collective-permute-start(f32[64,256]{1,0:T(8,128)S(1)} %get-tuple-element.79), channel_id=1, source_target_pairs={{0,4},{4,8},{8,12},{12,16},{16,20},{20,24},{24,28},{28,32},{32,36}... | collective-permute-start | bytes 196616 | tf_op jit(solution)/shard_map/ppermute | solution.py:272
  83.5 9.9 %collective-permute-start.29 = (f32[64,256]{1,0:T(8,128)S(1)}, f32[64,256]{1,0:T(8,128)S(1)}, u32[]{:S(2)}, u32[]{:S(2)}) collective-permute-start(f32[64,256]{1,0:T(8,128)S(1)} %get-tuple-element.80), channel_id=1, source_target_pairs={{0,252},{4,0},{8,4},{12,8},{16,12},{20,16},{24,20},{28,24},{32,28}... | collective-permute-start | bytes 196616 | tf_op jit(solution)/shard_map/ppermute | solution.py:273
  89.4 4.0 %collective-permute-start.30 = (f32[8,256]{1,0:T(8,128)S(1)}, f32[8,256]{1,0:T(8,128)S(1)}, u32[]{:S(2)}, u32[]{:S(2)}) collective-permute-start(f32[8,256]{1,0:T(8,128)S(1)} %get-tuple-element.81), channel_id=1, source_target_pairs={{0,1},{1,2},{2,3},{3,0},{4,5},{5,6},{6,7},{7,4},{8,9},{9,10},{10,1... | collective-permute-start | bytes 24584 | tf_op jit(solution)/shard_map/ppermute | solution.py:274
  90.5 2.9 %collective-permute-start.31 = (f32[8,256]{1,0:T(8,128)S(1)}, f32[8,256]{1,0:T(8,128)S(1)}, u32[]{:S(2)}, u32[]{:S(2)}) collective-permute-start(f32[8,256]{1,0:T(8,128)S(1)} %get-tuple-element.82), channel_id=1, source_target_pairs={{0,3},{1,0},{2,1},{3,2},{4,7},{5,4},{6,5},{7,6},{8,11},{9,8},{10,9... | collective-permute-start | bytes 24584 | tf_op jit(solution)/shard_map/ppermute | solution.py:275
where the time goes:
time: 125 us
  starting transfers between devices  70.1 us (56%)
  blocking collectives  25.3 us (20%)
  Pallas kernels  19.8 us (16%)
  waiting for transfers between devices  6.62 us (5%)
  local copies, waits for them, and re-layouts  1.64 us (1%)
    ppermute x8, starting transfers between devices, exchange(): lax.ppermute(x_low, GX, ring(nx, -1))  41.8 us
    all_to_all x1, blocking collectives, body(): lines = lax.all_to_all(line, EVERY, 0, 0, tiled=True)  25.3 us
    pallas_call x13, Pallas kernels, call(): pl.pallas_call(kernel, name=name, out_shape=outs, in_specs=specs, out_spe...  19.8 us
    ppermute x8, starting transfers between devices, exchange(): lax.ppermute(y_low, 'gy', ring(ny, -1))  15.5 us
    ppermute x8, starting transfers between devices, exchange(): lax.ppermute(y_high, 'gy', ring(ny, 1))  7.07 us
    ppermute x8, waiting for transfers between devices, exchange(): lax.ppermute(y_high, 'gy', ring(ny, 1))  6.11 us
    ppermute x8, starting transfers between devices, exchange(): lax.ppermute(x_high, GX, ring(nx, 1))  5.68 us
  transfers between devices with their start and end apart: 32, of which 8 were waited for; matrix products, arithmetic and copies ran while one was open for 1% of the time, Pallas kernels for 3%

commit v1 on v0

v1 whole, which is shorter than its diff:
```python
import functools

import jax
import jax.numpy as jnp
from jax import lax
from jax.experimental import pallas as pl
from jax.experimental.pallas import tpu as pltpu
from jax.sharding import Mesh
from jax.sharding import PartitionSpec as P

GX = ("gx_0", "gx_1", "gx_2")
EVERY = ("gx_0", "gx_1", "gx_2", "gy")
F32 = jnp.float32
GROWTH = 2.0
LIMIT = 8 * 1024 * 1024

VM = pl.BlockSpec(memory_space=pltpu.VMEM)
SM = pl.BlockSpec(memory_space=pltpu.SMEM)
ANY = pl.BlockSpec(memory_space=pl.ANY)


def on_chip(*shape):
    return pltpu.VMEM(shape, F32)


def pinned(array):
    return pltpu.with_memory_space_constraint(array, pltpu.VMEM)


def in_hbm(array):
    return pltpu.with_memory_space_constraint(array, pltpu.HBM)


def call(kernel, name, ins, specs, outs, out_specs=None, scratch=(), aliases=None):
    ins = [pinned(a) if s is VM else in_hbm(a) if s is ANY else a for a, s in zip(ins, specs)]
    return pl.pallas_call(
        kernel,
        name=name,
        out_shape=outs,
        in_specs=specs,
        out_specs=out_specs if out_specs is not None else [VM] * len(outs),
        scratch_shapes=scratch,
        input_output_aliases=aliases or {},
        compiler_params=pltpu.CompilerParams(vmem_limit_bytes=LIMIT),
    )(*ins)


G = 8


def run_copies(pairs, sems):
    copies = [pltpu.make_async_copy(s, t, sems.at[n]) for n, (s, t) in enumerate(pairs)]
    for copy in copies:
        copy.start()
    for copy in copies:
        copy.wait()


def cut_kernel(rhs, coefs, x_low, x_high, y_low, y_high, sems):
    planes, rows = rhs.shape[0], rhs.shape[1]
    pairs = [
        (rhs.at[0:2], x_low.at[0:2]),
        (coefs.at[0:7, 0], x_low.at[2:9]),
        (rhs.at[planes - 2 : planes], x_high.at[0:2]),
        (coefs.at[0:7, planes - 1], x_high.at[2:9]),
    ]
    for y, span in ((y_low, slice(0, G)), (y_high, slice(rows - G, rows))):
        for p in range(planes):
            pairs.append((rhs.at[p, span], y.at[0, G * p : G * p + G]))
            pairs.append((coefs.at[:, p, span], y.at[1:14, G * p : G * p + G]))
    run_copies(pairs, sems)


def load_kernel(rhs, coefs, after, field, own, sems):
    planes, rows = rhs.shape[0], rhs.shape[1]
    pairs = [(rhs, field.at[2 : planes + 2, G : rows + G])]
    for p in range(planes):
        pairs.append((coefs.at[:, p], own.at[:, rows * p : rows * p + rows]))
    run_copies(pairs, sems)


def relay_kernel(x_below, x_above, after, y_low, y_high):
    rows = x_below.shape[1]
    for n, x in enumerate((x_below, x_above)):
        y_low[n] = x[:, 0:G]
        y_high[n] = x[:, rows - G : rows]


def tile_at(row):
    return pl.ds(pl.multiple_of(row, 8), 8)


class Coefficients:
    def __init__(self, rows, own, y_below, y_above, corners=None):
        self.own, self.y_below, self.y_above, self.corners = own, y_below, y_above, corners
        self.rows, self.tiles = rows, rows // 8 + 2

    def spai(self, d, q, t):
        return self.plane(d, q, t)

    def oper(self, d, p, t):
        return self.plane(7 + d, p, t)

    def plane(self, d, p, t):
        if t == 0:
            return self.y_below[1 + d, tile_at(G * p), :]
        if t == self.tiles - 1:
            return self.y_above[1 + d, tile_at(G * p), :]
        return self.own[d, tile_at(self.rows * p + 8 * t - 8), :]

    def ghost(self, d, side, t):
        x, c_below, c_above = self.corners[side]
        if t == 0:
            return c_below[side, 2 + d]
        if t == self.tiles - 1:
            return c_above[side, 2 + d]
        return x[2 + d, 8 * t - 8 : 8 * t, :]


def edges():
    place = lax.axis_index("gy")
    last = lax.axis_size("gy") - 1
    return jnp.where(place > 0, 1.0, 0.0), jnp.where(place < last, 1.0, 0.0)


def within(edge, t, tiles, value):
    if t == 0:
        return value * edge[0]
    if t == tiles - 1:
        return value * edge[1]
    return value


def stencil(field, at, emit):
    tiles = field.shape[1] // 8
    lanes = field.shape[2]
    row = lax.broadcasted_iota(jnp.int32, (8, lanes), 0)
    lane = lax.broadcasted_iota(jnp.int32, (8, lanes), 1)
    top, bottom = row == 0, row == 7
    left, right = lane == 0, lane == lanes - 1

    def tile(t):
        value = field[at, 8 * t : 8 * t + 8, :]
        return value, pltpu.roll(value, 1, 0), pltpu.roll(value, 7, 0)

    before = here = tile(0)
    for t in range(tiles):
        after = tile(t + 1) if t + 1 < tiles else here
        value = here[0]
        span = slice(8 * t, 8 * t + 8)
        near = (
            field[at - 1, span, :],
            field[at + 1, span, :],
            jnp.where(top, before[1], here[1]),
            jnp.where(bottom, after[2], here[2]),
            jnp.where(left, 0.0, pltpu.roll(value, 1, 1)),
            jnp.where(right, 0.0, pltpu.roll(value, lanes - 1, 1)),
        )
        emit(t, span, value, near)
        before, here = here, after


def spai_plane(edge, coefficient, field, image, q):
    def emit(t, span, value, near):
        total = coefficient(0, t) * value
        for d in range(6):
            total = total + coefficient(1 + d, t) * near[d]
        image[q + 1, span, :] = within(edge, t, image.shape[1] // 8, total)

    stencil(field, q + 2, emit)


def oper_plane(edge, shift, coefs, field, image, out, p):
    def emit(t, span, value, near):
        total = value - shift * field[p + 2, span, :]
        for d in range(6):
            total = total - coefs.oper(d, p, t) * near[d]
        out[p + 2, span, :] = within(edge, t, out.shape[1] // 8, GROWTH * total)

    stencil(image, p + 1, emit)


def each(first, count, jump, work):
    half = count // 2

    def one(n, carry):
        work(first + n + jump * (n // half))
        return carry

    lax.fori_loop(0, count, one, 0)


def inner_work(shift, edge, coefs, field, image, out):
    planes = image.shape[0] - 2
    each(1, planes - 2, 0, lambda q: spai_plane(edge, lambda d, t: coefs.spai(d, q, t), field, image, q))
    each(2, planes - 4, 0, lambda p: oper_plane(edge, shift, coefs, field, image, out, p))


def outer_work(shift, edge, coefs, field, image, out):
    planes = image.shape[0] - 2
    for side, q in enumerate((-1, planes)):
        spai_plane(edge, lambda d, t: coefs.ghost(d, side, t), field, image, q)
    each(0, 2, planes - 2, lambda q: spai_plane(edge, lambda d, t: coefs.spai(d, q, t), field, image, q))
    each(0, 4, planes - 4, lambda p: oper_plane(edge, shift, coefs, field, image, out, p))


def send_edges(out, x_low, x_high):
    planes = out.shape[0] - 4
    x_low[...] = out[2:4]
    x_high[...] = out[planes : planes + 2]


def first_inner_kernel(shifts, own, y_below, y_above, field0, field, image, out):
    edge = edges()
    planes, tall = image.shape[0] - 2, image.shape[1]
    for p in range(planes):
        field[p + 2, 0:G, :] = y_below[0, G * p : G * p + G, :] * edge[0]
        field[p + 2, tall - G : tall, :] = y_above[0, G * p : G * p + G, :] * edge[1]
    inner_work(shifts[0], edge, Coefficients(field.shape[1] - 2 * G, own, y_below, y_above), field, image, out)


def inner_kernel(step, shifts, own, y_below, y_above, field, image, out):
    inner_work(shifts[step], edges(), Coefficients(field.shape[1] - 2 * G, own, y_below, y_above), field, image, out)


def outer_kernel(step, shifts, own, y_below, y_above, x_below, x_above, c_below, c_above, *refs):
    edge = edges()
    first = step == 0
    if first:
        field0, image0, out0, field, image, out, *sends = refs
    else:
        if step == 3:
            refs = refs[1:]
        v_below, v_above, field0, image0, out0, field, image, out, *sends = refs
    planes, tall = image.shape[0] - 2, image.shape[1]
    if first:
        for side, (x, at) in enumerate(((x_below, 0), (x_above, planes + 2))):
            field[at : at + 2, 0:G, :] = c_below[side, 0:2] * edge[0]
            field[at : at + 2, G : tall - G, :] = x[0:2]
            field[at : at + 2, tall - G : tall, :] = c_above[side, 0:2] * edge[1]
    else:
        field[0:2] = v_below[...]
        field[planes + 2 : planes + 4] = v_above[...]
    corners = ((x_below, c_below, c_above), (x_above, c_below, c_above))
    outer_work(shifts[step], edge, Coefficients(field.shape[1] - 2 * G, own, y_below, y_above, corners), field, image, out)
    if sends:
        send_edges(out, *sends)


def pair_rows(count):
    return [(i, j) for j in range(count) for i in range(j + 1)]


def gram_rows(fields, pairs, out, start):
    planes = fields[0].shape[0] - 4
    rows = fields[0].shape[1] - 2 * G

    def one(p, sums):
        sums = list(sums)
        for r in range(G, rows + G, 8):
            values = [f[p + 2, r : r + 8, :] for f in fields]
            for k, (i, j) in enumerate(pairs):
                sums[k] = sums[k] + values[i] * values[j]
        return tuple(sums)

    zero = jnp.zeros((8, fields[0].shape[2]), F32)
    sums = lax.fori_loop(0, planes, one, tuple(zero for _ in pairs))
    for k, s in enumerate(sums):
        out[start + k : start + k + 1, :] = jnp.sum(s[:, :128] + s[:, 128:], axis=0, keepdims=True)


def early_gram_kernel(v0, v1, v2, v3, out):
    out[...] = jnp.zeros_like(out)
    gram_rows((v0, v1, v2, v3), pair_rows(4), out, 0)


def late_gram_kernel(early, v0, v1, v2, v3, v4, out, hold):
    hold[...] = early[...]
    gram_rows((v0, v1, v2, v3, v4), [(i, 4) for i in range(5)], hold, 10)
    totals = jnp.sum(hold[...], axis=1, keepdims=True)
    row = lax.broadcasted_iota(jnp.int32, (16, 128), 0)
    lane = lax.broadcasted_iota(jnp.int32, (16, 128), 1)
    line = jnp.sum(jnp.where(row == lane, totals, 0.0), axis=0, keepdims=True)
    out[...] = jnp.broadcast_to(line, out.shape)


def solve(gram, shifts):
    n = 5
    zero = jnp.zeros_like(gram[0][0])
    one = jnp.ones_like(zero)
    lower = [[zero] * n for _ in range(n)]
    for j in range(n):
        rest = gram[j][j]
        for k in range(j):
            rest = rest - lower[j][k] * lower[j][k]
        pivot = jnp.sqrt(rest)
        lower[j][j] = pivot
        for i in range(j + 1, n):
            rest = gram[i][j]
            for k in range(j):
                rest = rest - lower[i][k] * lower[j][k]
            lower[i][j] = rest / pivot
    factor = [[lower[j][i] for j in range(n)] for i in range(n)]

    def invert(upper, order):
        result = [[zero] * order for _ in range(order)]
        for row in range(order - 1, -1, -1):
            for column in range(row, order):
                known = one if column == row else zero
                for k in range(row + 1, column + 1):
                    known = known - upper[row][k] * result[k][column]
                result[row][column] = known / upper[row][row]
        return result

    inverse = invert(factor, n)
    count = n - 1
    hess = [[None] * count for _ in range(n)]
    for row in range(n):
        for column in range(count):
            entry = zero
            if column >= row:
                entry = entry + factor[row][column] * shifts[column]
            if column + 1 >= row:
                entry = entry + factor[row][column + 1] * (1.0 / GROWTH)
            hess[row][column] = entry
    target = [factor[0][0]] + [zero] * (n - 1)
    for column in range(count):
        top, below = hess[column], hess[column + 1]
        radius = jnp.sqrt(top[column] * top[column] + below[column] * below[column])
        cosine = top[column] / radius
        sine = below[column] / radius
        hess[column] = [cosine * t + sine * b for t, b in zip(top, below)]
        hess[column + 1] = [cosine * b - sine * t for t, b in zip(top, below)]
        first, second = target[column], target[column + 1]
        target[column] = cosine * first + sine * second
        target[column + 1] = cosine * second - sine * first
    upper_inverse = invert(hess, count)
    weights = []
    for row in range(count):
        entry = zero
        for k in range(row, count):
            entry = entry + upper_inverse[row][k] * target[k]
        weights.append(entry)
    combine = []
    for row in range(n):
        entry = one if row == 0 else zero
        if row < count:
            entry = entry - shifts[row] * weights[row]
        if row > 0:
            entry = entry - (1.0 / GROWTH) * weights[row - 1]
        combine.append(entry)
    return factor, inverse, weights, combine


def final_kernel(cells, shifts, rows, v0, v1, v2, v3, v4, w0, w1, w2, w3,
                 basis, factor_out, solution_out, residual_out, made, sems):
    line = jnp.sum(rows[...], axis=0, keepdims=True) * (1.0 / cells)
    gram = [[None] * 5 for _ in range(5)]
    for k, (i, j) in enumerate(pair_rows(5)):
        entry = jnp.broadcast_to(line[:, k : k + 1], (8, 128))
        gram[i][j] = entry
        gram[j][i] = entry
    factor, inverse, weights, combine = solve(gram, [shifts[k] for k in range(4)])
    row = lax.broadcasted_iota(jnp.int32, (8, 128), 0)
    lane = lax.broadcasted_iota(jnp.int32, (8, 128), 1)
    table = jnp.zeros((8, 128), F32)
    for i in range(5):
        for j in range(i, 5):
            table = jnp.where((row == i) & (lane == j), factor[i][j], table)
    factor_out[...] = table[:5, :5]
    fields = (v0, v1, v2, v3, v4)
    images = (w0, w1, w2, w3)
    planes = made.shape[1]

    def copies(p):
        triples = ((made.at[0:5, p], basis.at[:, p]), (made.at[5, p], solution_out.at[p]), (made.at[6, p], residual_out.at[p]))
        return [pltpu.make_async_copy(source, target, sems.at[p, n]) for n, (source, target) in enumerate(triples)]

    def one(p, carry):
        for r in range(0, made.shape[2], 8):
            for c in range(0, made.shape[3], 128):
                v = [f[p + 2, r + G : r + G + 8, c : c + 128] for f in fields]
                w = [f[p + 1, r + G : r + G + 8, c : c + 128] for f in images]
                for k in range(5):
                    total = inverse[0][k] * v[0]
                    for j in range(1, k + 1):
                        total = total + inverse[j][k] * v[j]
                    made[k, p, r : r + 8, c : c + 128] = total
                total = weights[0] * w[0]
                for k in range(1, 4):
                    total = total + weights[k] * w[k]
                made[5, p, r : r + 8, c : c + 128] = total
                total = combine[0] * v[0]
                for j in range(1, 5):
                    total = total + combine[j] * v[j]
                made[6, p, r : r + 8, c : c + 128] = total
        for copy in copies(p):
            copy.start()
        return carry

    def finish(p, carry):
        for copy in copies(p):
            copy.wait()
        return carry

    lax.fori_loop(0, planes, one, 0)
    lax.fori_loop(0, planes, finish, 0)


def ring(count, step):
    return [(i, (i + step) % count) for i in range(count)]


def both_ways(low, high, axis):
    count = lax.axis_size(axis)
    return lax.ppermute(high, axis, ring(count, 1)), lax.ppermute(low, axis, ring(count, -1))


def body(rhs, coefs, shifts):
    planes, rows, lanes = rhs.shape
    tall = rows + 2 * G
    field = on_chip(planes + 4, tall, lanes)
    image = on_chip(planes + 2, tall, lanes)
    halo = on_chip(2, tall, lanes)
    x_cut, y_cut = on_chip(9, rows, lanes), on_chip(14, G * planes, lanes)
    corner = on_chip(2, 9, G, lanes)
    x_low, x_high, y_low, y_high = call(
        cut_kernel, "cut", [rhs, coefs], [ANY] * 2, [x_cut, x_cut, y_cut, y_cut],
        scratch=[pltpu.SemaphoreType.DMA((4 + 4 * planes,))],
    )
    x_below, x_above = both_ways(x_low, x_high, GX)
    y_below, y_above = both_ways(y_low, y_high, "gy")
    v, own = call(
        load_kernel, "load", [rhs, coefs, y_low], [ANY, ANY, VM], [field, on_chip(13, planes * rows, lanes)],
        scratch=[pltpu.SemaphoreType.DMA((1 + planes,))],
    )
    c_low, c_high = call(relay_kernel, "relay", [x_below, x_above, own], [VM] * 3, [corner, corner])
    c_below, c_above = both_ways(c_low, c_high, "gy")
    basis, images = [], []
    for step in range(4):
        common = [shifts, own, y_below, y_above]
        specs = [SM] + [VM] * 3
        if step == 0:
            v, w, out = call(
                first_inner_kernel, "first_inner", common + [v], specs + [VM], [field, image, field], aliases={4: 0}
            )
        else:
            w, out = call(functools.partial(inner_kernel, step), "inner", common + [v], specs + [VM], [image, field])
        common += [x_below, x_above, c_below, c_above]
        if step == 3:
            (early,) = call(early_gram_kernel, "early_gram", basis + [v], [VM] * 4, [on_chip(16, 128)])
            common += [early]
        common += [] if step == 0 else [below, above]
        specs += [VM] * (len(common) - 4)
        at = len(common)
        v, w, out, *sends = call(
            functools.partial(outer_kernel, step),
            "first_outer" if step == 0 else "outer",
            common + [v, w, out], specs + [VM] * 3,
            [field, image, field] + [halo, halo] * (step < 3), aliases={at: 0, at + 1: 1, at + 2: 2},
        )
        if sends:
            below, above = both_ways(*sends, GX)
        basis.append(v)
        images.append(w)
        v = out
    basis.append(v)
    devices = lax.axis_size(GX) * lax.axis_size("gy")
    (line,) = call(
        late_gram_kernel, "late_gram", [early, *basis], [VM] * 6, [on_chip(devices, 128)],
        scratch=[pltpu.VMEM((16, 128), F32)],
    )
    lines = lax.all_to_all(line, EVERY, 0, 0, tiled=True)
    cells = float(planes * rows * lanes * devices)
    whole = jax.ShapeDtypeStruct((planes, rows, lanes), F32)
    return tuple(
        call(
            lambda *refs: final_kernel(cells, *refs), "final",
            [shifts, lines, *basis, *images], [SM] + [VM] * 10,
            [jax.ShapeDtypeStruct((5, planes, rows, lanes), F32), jax.ShapeDtypeStruct((5, 5), F32), whole, whole],
            out_specs=[ANY, VM, ANY, ANY],
            scratch=[pltpu.VMEM((7, planes, rows, lanes), F32), pltpu.SemaphoreType.DMA((planes, 3))],
        )
    )


def solution(mesh):
    torus = Mesh(mesh.devices.reshape(4, 8, 2, mesh.shape["gy"]), EVERY)
    in_specs = (P(GX, "gy", None), P(None, GX, "gy", None), P())
    out_specs = (P(None, GX, "gy", None), P(), P(GX, "gy", None), P(GX, "gy", None))
    return jax.shard_map(body, mesh=torus, in_specs=in_specs, out_specs=out_specs, check_vma=False)
```

time: 125 us -> 88.8 us (0.71)
  starting transfers between devices: 70.1 us -> 23.3 us
  waiting for transfers between devices: 6.62 us -> 14.5 us
  Pallas kernels: 19.8 us -> 22.5 us
  blocking collectives: 25.3 us -> 27.5 us
  local copies, waits for them, and re-layouts: 1.64 us -> 0.01 us
    ppermute x32 -> x12, starting transfers between devices: 70.1 us -> 23.3 us  [the longest x6 14.2 us: both_ways(): lax.ppermute(low, axis, ring(count, -1))]
    ppermute x32 -> x12, waiting for transfers between devices: 6.62 us -> 14.5 us  [the longest x6 8.15 us: both_ways(): lax.ppermute(low, axis, ring(count, -1))]
    pallas_call x13 -> x14, Pallas kernels: 19.8 us -> 22.5 us  [call(): pl.pallas_call(kernel, name=name, out_shape=outs, in_specs=specs, out_spe...]
    all_to_all x1, blocking collectives: 25.3 us -> 27.5 us  [body(): lines = lax.all_to_all(line, EVERY, 0, 0, tiled=True)]
  transfers between devices with their start and end apart: 32 -> 12, of which waited for: 8 -> 7; matrix products, arithmetic and copies ran while one was open for 1% -> 0% of each run, Pallas kernels for 3% -> 12%
where the time goes in v1:
time: 88.8 us; the launch traced here: 88.7 us
  blocking collectives  27.5 us (31%)
  starting transfers between devices  23.3 us (26%)
  Pallas kernels  22.5 us (25%)
  waiting for transfers between devices  14.5 us (16%)
    all_to_all x1, blocking collectives, body(): lines = lax.all_to_all(line, EVERY, 0, 0, tiled=True)  27.5 us
    pallas_call x14, Pallas kernels, call(): pl.pallas_call(kernel, name=name, out_shape=outs, in_specs=specs, out_spe...  22.5 us
    ppermute x6, starting transfers between devices, both_ways(): lax.ppermute(low, axis, ring(count, -1))  14.2 us
    ppermute x6, starting transfers between devices, both_ways(): lax.ppermute(high, axis, ring(count, 1))  9.14 us
    ppermute x6, waiting for transfers between devices, both_ways(): lax.ppermute(low, axis, ring(count, -1))  8.15 us
    ppermute x6, waiting for transfers between devices, both_ways(): lax.ppermute(high, axis, ring(count, 1))  6.37 us
  transfers between devices with their start and end apart: 12, of which 7 were waited for; matrix products, arithmetic and copies ran while one was open for 0% of the time, Pallas kernels for 12%

profile of v1, /device:TPU:1, one launch (start us, length us, event | category | flops | bytes accessed | tf_op | source)
XLA Modules:
  0.0 88.7 jit_solution(9039368416900298762)
XLA Ops:
  0.6 2.2 %cut.1 = (f32[9,64,256]{2,1,0:T(8,128)S(1)}, f32[9,64,256]{2,1,0:T(8,128)S(1)}, f32[14,64,256]{2,1,0:T(8,128)S(1)}, f32[14,64,256]{2,1,0:T(8,128)S(1)}) custom-call(f32[8,64,256]{2,1,0:T(8,128)} %rhs.3, f32[13,8,64,256]{3,2,1,0:T(8,128)} %coefs.3), custom_call_target="tpu_custom_call" | custom-call | tf_op jit(solution)/shard_map/cut/pallas_call | solution.py:36
  2.8 2.1 %collective-permute-start = (f32[14,64,256]{2,1,0:T(8,128)S(1)}, f32[14,64,256]{2,1,0:T(8,128)S(1)}, u32[]{:S(2)}, u32[]{:S(2)}) collective-permute-start(f32[14,64,256]{2,1,0:T(8,128)S(1)} %get-tuple-element.41), channel_id=1, source_target_pairs={{0,1},{1,2},{2,3},{3,0},{4,5},{5,6},{6,7},{7,4},{8,9},{9,10},{10,1... | collective-permute-start | bytes 2752520 | tf_op jit(solution)/shard_map/ppermute | solution.py:416
  4.9 1.4 %collective-permute-start.1 = (f32[14,64,256]{2,1,0:T(8,128)S(1)}, f32[14,64,256]{2,1,0:T(8,128)S(1)}, u32[]{:S(2)}, u32[]{:S(2)}) collective-permute-start(f32[14,64,256]{2,1,0:T(8,128)S(1)} %get-tuple-element.39.after), channel_id=1, source_target_pairs={{0,3},{1,0},{2,1},{3,2},{4,7},{5,4},{6,5},{7,6},{8,11},{9,8},{10,9... | collective-permute-start | bytes 2752520 | tf_op jit(solution)/shard_map/ppermute | solution.py:416
  6.3 2.9 %collective-permute-start.2 = (f32[9,64,256]{2,1,0:T(8,128)S(1)}, f32[9,64,256]{2,1,0:T(8,128)S(1)}, u32[]{:S(2)}, u32[]{:S(2)}) collective-permute-start(f32[9,64,256]{2,1,0:T(8,128)S(1)} %get-tuple-element.42), channel_id=1, source_target_pairs={{0,4},{4,8},{8,12},{12,16},{16,20},{20,24},{24,28},{28,32},{32,36}... | collective-permute-start | bytes 1769480 | tf_op jit(solution)/shard_map/ppermute | solution.py:416
  9.2 0.0 copy-start
  9.2 0.2 collective-permute-start.3
  9.4 3.2 %load.1 = (f32[12,80,256]{2,1,0:T(8,128)S(1)}, f32[13,512,256]{2,1,0:T(8,128)S(1)}) custom-call(f32[8,64,256]{2,1,0:T(8,128)} %rhs.3, f32[13,8,64,256]{3,2,1,0:T(8,128)} %coefs.3, f32[14,64,256]{2,1,0:T(8,128)S(1)} %get-tuple-element.39.after), custom_call_target="tpu_custom_call" | custom-call | tf_op jit(solution)/shard_map/load/pallas_call | solution.py:36
  12.6 3.4 %collective-permute-done.2.x_below = f32[9,64,256]{2,1,0:T(8,128)S(1)} collective-permute-done((f32[9,64,256]{2,1,0:T(8,128)S(1)}, f32[9,64,256]{2,1,0:T(8,128)S(1)}, u32[]{:S(2)}, u32[]{:S(2)}) %collective-permute-start.2) | collective-permute-done | bytes 589856 | tf_op jit(solution)/shard_map/ppermute | solution.py:416
  16.0 2.8 %collective-permute-done.3.x_above = f32[9,64,256]{2,1,0:T(8,128)S(1)} collective-permute-done((f32[9,64,256]{2,1,0:T(8,128)S(1)}, f32[9,64,256]{2,1,0:T(8,128)S(1)}, u32[]{:S(2)}, u32[]{:S(2)}) %collective-permute-start.3) | collective-permute-done | bytes 589856 | tf_op jit(solution)/shard_map/ppermute | solution.py:416
  18.8 0.1 collective-permute-start.4
  18.9 2.7 %collective-permute-start.5 = (f32[2,9,8,256]{3,2,1,0:T(8,128)S(1)}, f32[2,9,8,256]{3,2,1,0:T(8,128)S(1)}, u32[]{:S(2)}, u32[]{:S(2)}) collective-permute-start(f32[2,9,8,256]{3,2,1,0:T(8,128)S(1)} %get-tuple-element.45), channel_id=1, source_target_pairs={{0,3},{1,0},{2,1},{3,2},{4,7},{5,4},{6,5},{7,6},{8,11},{9,8},{10,9... | collective-permute-start | bytes 442376 | tf_op jit(solution)/shard_map/ppermute | solution.py:416
  21.6 2.4 %collective-permute-done.y_below = f32[14,64,256]{2,1,0:T(8,128)S(1)} collective-permute-done((f32[14,64,256]{2,1,0:T(8,128)S(1)}, f32[14,64,256]{2,1,0:T(8,128)S(1)}, u32[]{:S(2)}, u32[]{:S(2)}) %collective-permute-start) | collective-permute-done | bytes 917536 | tf_op jit(solution)/shard_map/ppermute | solution.py:416
  24.0 1.5 %collective-permute-done.1.y_above = f32[14,64,256]{2,1,0:T(8,128)S(1)} collective-permute-done((f32[14,64,256]{2,1,0:T(8,128)S(1)}, f32[14,64,256]{2,1,0:T(8,128)S(1)}, u32[]{:S(2)}, u32[]{:S(2)}) %collective-permute-start.1) | collective-permute-done | bytes 917536 | tf_op jit(solution)/shard_map/ppermute | solution.py:416
  25.5 0.0 copy-done
  25.5 1.8 %first_inner.1 = (f32[12,80,256]{2,1,0:T(8,128)S(1)}, f32[10,80,256]{2,1,0:T(8,128)S(1)}, f32[12,80,256]{2,1,0:T(8,128)S(1)}) custom-call(f32[4]{0:T(128)S(1)} %copy-done, f32[13,512,256]{2,1,0:T(8,128)S(1)} %get-tuple-element.40.after.own, f32[14,64,256]{2,1,0:T(8,128)S(1)} %collective-permute-done.y_below, ...), custom_call_target="tpu_custom_call", output_to_operand_aliasing={{0}: (4, {})} | custom-call | tf_op jit(solution)/shard_map/first_inner/pallas_call | solution.py:36
  27.3 0.0 collective-permute-done.4.c_below
  27.3 1.4 %collective-permute-done.5.c_above = f32[2,9,8,256]{3,2,1,0:T(8,128)S(1)} collective-permute-done((f32[2,9,8,256]{3,2,1,0:T(8,128)S(1)}, f32[2,9,8,256]{3,2,1,0:T(8,128)S(1)}, u32[]{:S(2)}, u32[]{:S(2)}) %collective-permute-start.5) | collective-permute-done | bytes 147488 | tf_op jit(solution)/shard_map/ppermute | solution.py:416
  28.7 1.5 %first_outer.1 = (f32[12,80,256]{2,1,0:T(8,128)S(1)}, f32[10,80,256]{2,1,0:T(8,128)S(1)}, f32[12,80,256]{2,1,0:T(8,128)S(1)}, f32[2,80,256]{2,1,0:T(8,128)S(1)}, f32[2,80,256]{2,1,0:T(8,128)S(1)}) custom-call(f32[4]{0:T(128)S(1)} %copy-done, ...), custom_call_target="tpu_custom_call", output_to_operand_aliasing={{0}: (8, {}), {1}: (9, {}), {2}: (10, {})} | custom-call | tf_op jit(solution)/shard_map/first_outer/pallas_call | solution.py:36
  30.1 3.9 %collective-permute-start.6 = (f32[2,80,256]{2,1,0:T(8,128)S(1)}, f32[2,80,256]{2,1,0:T(8,128)S(1)}, u32[]{:S(2)}, u32[]{:S(2)}) collective-permute-start(f32[2,80,256]{2,1,0:T(8,128)S(1)} %get-tuple-element.51), channel_id=1, source_target_pairs={{0,4},{4,8},{8,12},{12,16},{16,20},{20,24},{24,28},{28,32},{32,36}... | collective-permute-start | bytes 491528 | tf_op jit(solution)/shard_map/ppermute | solution.py:416
  34.0 0.0 collective-permute-start.7
  34.1 1.8 %inner.3 = (f32[10,80,256]{2,1,0:T(8,128)S(1)}, f32[12,80,256]{2,1,0:T(8,128)S(1)}) custom-call(f32[4]{0:T(128)S(1)} %copy-done, f32[13,512,256]{2,1,0:T(8,128)S(1)} %get-tuple-element.40.after.own, f32[14,64,256]{2,1,0:T(8,128)S(1)} %collective-permute-done.y_below, f32[14,64,256]{2,1,0:T(8,128)S(1)} %collective-permute-done.1.y_above, ...), custom_call_target="tpu_custom_call" | custom-call | tf_op jit(solution)/shard_map/inner/pallas_call | solution.py:36
  35.8 0.5 collective-permute-done.6.refs_0_
  36.3 2.5 %collective-permute-done.7.refs_1_ = f32[2,80,256]{2,1,0:T(8,128)S(1)} collective-permute-done((f32[2,80,256]{2,1,0:T(8,128)S(1)}, f32[2,80,256]{2,1,0:T(8,128)S(1)}, u32[]{:S(2)}, u32[]{:S(2)}) %collective-permute-start.7) | collective-permute-done | bytes 163872 | tf_op jit(solution)/shard_map/ppermute | solution.py:416
  38.8 1.5 %outer.3 = (f32[12,80,256]{2,1,0:T(8,128)S(1)}, f32[10,80,256]{2,1,0:T(8,128)S(1)}, f32[12,80,256]{2,1,0:T(8,128)S(1)}, f32[2,80,256]{2,1,0:T(8,128)S(1)}, f32[2,80,256]{2,1,0:T(8,128)S(1)}) custom-call(f32[4]{0:T(128)S(1)} %copy-done, ...), custom_call_target="tpu_custom_call", output_to_operand_aliasing={{0}: (10, {}), {1}: (11, {}), {2}: (12, {})} | custom-call | tf_op jit(solution)/shard_map/outer/pallas_call | solution.py:36
  40.3 0.1 collective-permute-start.8
  40.4 3.6 %collective-permute-start.9 = (f32[2,80,256]{2,1,0:T(8,128)S(1)}, f32[2,80,256]{2,1,0:T(8,128)S(1)}, u32[]{:S(2)}, u32[]{:S(2)}) collective-permute-start(f32[2,80,256]{2,1,0:T(8,128)S(1)} %get-tuple-element.58), channel_id=1, source_target_pairs={{0,252},{4,0},{8,4},{12,8},{16,12},{20,16},{24,20},{28,24},{32,28}... | collective-permute-start | bytes 491528 | tf_op jit(solution)/shard_map/ppermute | solution.py:416
  44.0 1.8 %inner.4 = (f32[10,80,256]{2,1,0:T(8,128)S(1)}, f32[12,80,256]{2,1,0:T(8,128)S(1)}) custom-call(f32[4]{0:T(128)S(1)} %copy-done, f32[13,512,256]{2,1,0:T(8,128)S(1)} %get-tuple-element.40.after.own, f32[14,64,256]{2,1,0:T(8,128)S(1)} %collective-permute-done.y_below, f32[14,64,256]{2,1,0:T(8,128)S(1)} %collective-permute-done.1.y_above, ...), custom_call_target="tpu_custom_call" | custom-call | tf_op jit(solution)/shard_map/inner/pallas_call | solution.py:36
  45.7 0.0 collective-permute-done.8.refs_0_
  45.7 0.0 collective-permute-done.9.refs_1_
  45.7 1.5 %outer.4 = (f32[12,80,256]{2,1,0:T(8,128)S(1)}, f32[10,80,256]{2,1,0:T(8,128)S(1)}, f32[12,80,256]{2,1,0:T(8,128)S(1)}, f32[2,80,256]{2,1,0:T(8,128)S(1)}, f32[2,80,256]{2,1,0:T(8,128)S(1)}) custom-call(f32[4]{0:T(128)S(1)} %copy-done, ...), custom_call_target="tpu_custom_call", output_to_operand_aliasing={{0}: (10, {}), {1}: (11, {}), {2}: (12, {})} | custom-call | tf_op jit(solution)/shard_map/outer/pallas_call | solution.py:36
  47.2 0.1 collective-permute-start.10
  47.3 6.3 %collective-permute-start.11 = (f32[2,80,256]{2,1,0:T(8,128)S(1)}, f32[2,80,256]{2,1,0:T(8,128)S(1)}, u32[]{:S(2)}, u32[]{:S(2)}) collective-permute-start(f32[2,80,256]{2,1,0:T(8,128)S(1)} %get-tuple-element.65), channel_id=1, source_target_pairs={{0,252},{4,0},{8,4},{12,8},{16,12},{20,16},{24,20},{28,24},{32,28}... | collective-permute-start | bytes 491528 | tf_op jit(solution)/shard_map/ppermute | solution.py:416
  53.7 0.4 early_gram.1.refs_0_.early
  54.1 1.8 %inner.5 = (f32[10,80,256]{2,1,0:T(8,128)S(1)}, f32[12,80,256]{2,1,0:T(8,128)S(1)}) custom-call(f32[4]{0:T(128)S(1)} %copy-done, f32[13,512,256]{2,1,0:T(8,128)S(1)} %get-tuple-element.40.after.own, f32[14,64,256]{2,1,0:T(8,128)S(1)} %collective-permute-done.y_below, f32[14,64,256]{2,1,0:T(8,128)S(1)} %collective-permute-done.1.y_above, ...), custom_call_target="tpu_custom_call" | custom-call | tf_op jit(solution)/shard_map/inner/pallas_call | solution.py:36
  55.9 0.0 collective-permute-done.10.refs_1_
  55.9 0.0 collective-permute-done.11.refs_2_
  55.9 1.5 %outer.5 = (f32[12,80,256]{2,1,0:T(8,128)S(1)}, f32[10,80,256]{2,1,0:T(8,128)S(1)}, f32[12,80,256]{2,1,0:T(8,128)S(1)}) custom-call(f32[4]{0:T(128)S(1)} %copy-done, f32[13,512,256]{2,1,0:T(8,128)S(1)} %get-tuple-element.40.after.own, f32[14,64,256]{2,1,0:T(8,128)S(1)} %collective-permute-done.y_below, ...), custom_call_target="tpu_custom_call", output_to_operand_aliasing={{0}: (11, {}), {1}: (12, {}), {2}: (13, {})} | custom-call | tf_op jit(solution)/shard_map/outer/pallas_call | solution.py:36
  57.4 0.3 late_gram.1
  57.7 27.5 %all_to_all.11 = f32[256,1,128]{2,1,0:T(1,128)S(1)} all-to-all(f32[256,1,128]{2,1,0:T(1,128)S(1)} %bitcast.5), channel_id=1, replica_groups=mesh['gx_0'=4,'gx_1'=8,'gx_2'=2,'gy'=4] {'gx_0','gx_1','gx_2','gy'}, dimensions={0} | all-to-all | bytes 262144 | tf_op jit(solution)/shard_map/all_to_all | solution.py:473
  85.2 3.5 %final.1 = (f32[5,8,64,256]{3,2,1,0:T(8,128)}, f32[5,5]{1,0:T(8,128)}, f32[8,64,256]{2,1,0:T(8,128)}, f32[8,64,256]{2,1,0:T(8,128)}) custom-call(f32[4]{0:T(128)S(1)} %copy-done, f32[256,128]{1,0:T(8,128)S(1)} %bitcast.4, f32[12,80,256]{2,1,0:T(8,128)S(1)} %get-tuple-element.50.v0.refs_2_, f32[12,80,256]{2,1,0:T(8,128)S(1)} %get-tuple-element.56.v1.refs_3_, ...), custom_call_target="tpu_custom_call" | custom-call | tf_op jit(solution)/shard_map/final/pallas_call | solution.py:36
  (1 shorter events, 0.0 us)
Async XLA Ops:
  2.8 21.2 %collective-permute-start = (f32[14,64,256]{2,1,0:T(8,128)S(1)}, f32[14,64,256]{2,1,0:T(8,128)S(1)}, u32[]{:S(2)}, u32[]{:S(2)}) collective-permute-start(f32[14,64,256]{2,1,0:T(8,128)S(1)} %get-tuple-element.41), channel_id=1, source_target_pairs={{0,1},{1,2},{2,3},{3,0},{4,5},{5,6},{6,7},{7,4},{8,9},{9,10},{10,1... | collective-permute-start | bytes 2752520 | tf_op jit(solution)/shard_map/ppermute | solution.py:416
  4.9 20.5 %collective-permute-start.1 = (f32[14,64,256]{2,1,0:T(8,128)S(1)}, f32[14,64,256]{2,1,0:T(8,128)S(1)}, u32[]{:S(2)}, u32[]{:S(2)}) collective-permute-start(f32[14,64,256]{2,1,0:T(8,128)S(1)} %get-tuple-element.39.after), channel_id=1, source_target_pairs={{0,3},{1,0},{2,1},{3,2},{4,7},{5,4},{6,5},{7,6},{8,11},{9,8},{10,9... | collective-permute-start | bytes 2752520 | tf_op jit(solution)/shard_map/ppermute | solution.py:416
  6.3 9.7 %collective-permute-start.2 = (f32[9,64,256]{2,1,0:T(8,128)S(1)}, f32[9,64,256]{2,1,0:T(8,128)S(1)}, u32[]{:S(2)}, u32[]{:S(2)}) collective-permute-start(f32[9,64,256]{2,1,0:T(8,128)S(1)} %get-tuple-element.42), channel_id=1, source_target_pairs={{0,4},{4,8},{8,12},{12,16},{16,20},{20,24},{24,28},{28,32},{32,36}... | collective-permute-start | bytes 1769480 | tf_op jit(solution)/shard_map/ppermute | solution.py:416
  9.2 16.3 %copy-start = (f32[4]{0:T(128)S(1)}, f32[4]{0:T(128)}, u32[]{:S(2)}) copy-start(f32[4]{0:T(128)} %refs_0_.1) | copy-start | bytes 52
  9.2 9.6 %collective-permute-start.3 = (f32[9,64,256]{2,1,0:T(8,128)S(1)}, f32[9,64,256]{2,1,0:T(8,128)S(1)}, u32[]{:S(2)}, u32[]{:S(2)}) collective-permute-start(f32[9,64,256]{2,1,0:T(8,128)S(1)} %get-tuple-element.43), channel_id=1, source_target_pairs={{0,252},{4,0},{8,4},{12,8},{16,12},{20,16},{24,20},{28,24},{32,28}... | collective-permute-start | bytes 1769480 | tf_op jit(solution)/shard_map/ppermute | solution.py:416
  18.8 8.5 %collective-permute-start.4 = (f32[2,9,8,256]{3,2,1,0:T(8,128)S(1)}, f32[2,9,8,256]{3,2,1,0:T(8,128)S(1)}, u32[]{:S(2)}, u32[]{:S(2)}) collective-permute-start(f32[2,9,8,256]{3,2,1,0:T(8,128)S(1)} %get-tuple-element.44), channel_id=1, source_target_pairs={{0,1},{1,2},{2,3},{3,0},{4,5},{5,6},{6,7},{7,4},{8,9},{9,10},{10,1... | collective-permute-start | bytes 442376 | tf_op jit(solution)/shard_map/ppermute | solution.py:416
  18.9 9.8 %collective-permute-start.5 = (f32[2,9,8,256]{3,2,1,0:T(8,128)S(1)}, f32[2,9,8,256]{3,2,1,0:T(8,128)S(1)}, u32[]{:S(2)}, u32[]{:S(2)}) collective-permute-start(f32[2,9,8,256]{3,2,1,0:T(8,128)S(1)} %get-tuple-element.45), channel_id=1, source_target_pairs={{0,3},{1,0},{2,1},{3,2},{4,7},{5,4},{6,5},{7,6},{8,11},{9,8},{10,9... | collective-permute-start | bytes 442376 | tf_op jit(solution)/shard_map/ppermute | solution.py:416
  30.1 6.2 %collective-permute-start.6 = (f32[2,80,256]{2,1,0:T(8,128)S(1)}, f32[2,80,256]{2,1,0:T(8,128)S(1)}, u32[]{:S(2)}, u32[]{:S(2)}) collective-permute-start(f32[2,80,256]{2,1,0:T(8,128)S(1)} %get-tuple-element.51), channel_id=1, source_target_pairs={{0,4},{4,8},{8,12},{12,16},{16,20},{20,24},{24,28},{28,32},{32,36}... | collective-permute-start | bytes 491528 | tf_op jit(solution)/shard_map/ppermute | solution.py:416
  34.0 4.7 %collective-permute-start.7 = (f32[2,80,256]{2,1,0:T(8,128)S(1)}, f32[2,80,256]{2,1,0:T(8,128)S(1)}, u32[]{:S(2)}, u32[]{:S(2)}) collective-permute-start(f32[2,80,256]{2,1,0:T(8,128)S(1)} %get-tuple-element.52), channel_id=1, source_target_pairs={{0,252},{4,0},{8,4},{12,8},{16,12},{20,16},{24,20},{28,24},{32,28}... | collective-permute-start | bytes 491528 | tf_op jit(solution)/shard_map/ppermute | solution.py:416
  40.3 5.5 %collective-permute-start.8 = (f32[2,80,256]{2,1,0:T(8,128)S(1)}, f32[2,80,256]{2,1,0:T(8,128)S(1)}, u32[]{:S(2)}, u32[]{:S(2)}) collective-permute-start(f32[2,80,256]{2,1,0:T(8,128)S(1)} %get-tuple-element.57), channel_id=1, source_target_pairs={{0,4},{4,8},{8,12},{12,16},{16,20},{20,24},{24,28},{28,32},{32,36}... | collective-permute-start | bytes 491528 | tf_op jit(solution)/shard_map/ppermute | solution.py:416
  40.4 5.4 %collective-permute-start.9 = (f32[2,80,256]{2,1,0:T(8,128)S(1)}, f32[2,80,256]{2,1,0:T(8,128)S(1)}, u32[]{:S(2)}, u32[]{:S(2)}) collective-permute-start(f32[2,80,256]{2,1,0:T(8,128)S(1)} %get-tuple-element.58), channel_id=1, source_target_pairs={{0,252},{4,0},{8,4},{12,8},{16,12},{20,16},{24,20},{28,24},{32,28}... | collective-permute-start | bytes 491528 | tf_op jit(solution)/shard_map/ppermute | solution.py:416
  47.2 8.6 %collective-permute-start.10 = (f32[2,80,256]{2,1,0:T(8,128)S(1)}, f32[2,80,256]{2,1,0:T(8,128)S(1)}, u32[]{:S(2)}, u32[]{:S(2)}) collective-permute-start(f32[2,80,256]{2,1,0:T(8,128)S(1)} %get-tuple-element.64), channel_id=1, source_target_pairs={{0,4},{4,8},{8,12},{12,16},{16,20},{20,24},{24,28},{28,32},{32,36}... | collective-permute-start | bytes 491528 | tf_op jit(solution)/shard_map/ppermute | solution.py:416
  47.3 8.5 %collective-permute-start.11 = (f32[2,80,256]{2,1,0:T(8,128)S(1)}, f32[2,80,256]{2,1,0:T(8,128)S(1)}, u32[]{:S(2)}, u32[]{:S(2)}) collective-permute-start(f32[2,80,256]{2,1,0:T(8,128)S(1)} %get-tuple-element.65), channel_id=1, source_target_pairs={{0,252},{4,0},{8,4},{12,8},{16,12},{20,16},{24,20},{28,24},{32,28}... | collective-permute-start | bytes 491528 | tf_op jit(solution)/shard_map/ppermute | solution.py:416

commit v2 on v1

--- a/solution.py
+++ b/solution.py
@@ -56,65 +56,54 @@
         copy.wait()
 
 
-def cut_kernel(rhs, coefs, x_low, x_high, y_low, y_high, sems):
+EARLY = 4
+
+
+def cut_rows_kernel(rhs, coefs, y_low, y_high, sems):
     planes, rows = rhs.shape[0], rhs.shape[1]
-    pairs = [
-        (rhs.at[0:2], x_low.at[0:2]),
-        (coefs.at[0:7, 0], x_low.at[2:9]),
-        (rhs.at[planes - 2 : planes], x_high.at[0:2]),
-        (coefs.at[0:7, planes - 1], x_high.at[2:9]),
-    ]
+    pairs = []
     for y, span in ((y_low, slice(0, G)), (y_high, slice(rows - G, rows))):
-        for p in range(planes):
-            pairs.append((rhs.at[p, span], y.at[0, G * p : G * p + G]))
-            pairs.append((coefs.at[:, p, span], y.at[1:14, G * p : G * p + G]))
+        pairs.append((rhs.at[:, span], y.at[0:planes]))
+        pairs.append((coefs.at[0:7, 0, span], y.at[planes : planes + 7]))
+        pairs.append((coefs.at[0:7, planes - 1, span], y.at[planes + 7 : planes + 14]))
+        for d in range(EARLY):
+            at = planes + 14 + (planes - 2) * d
+            pairs.append((coefs.at[d, 1 : planes - 1, span], y.at[at : at + planes - 2]))
+    run_copies(pairs, sems)
+
+
+def cut_rest_kernel(coefs, after, y_low, y_high, sems):
+    planes, rows = coefs.shape[1], coefs.shape[2]
+    pairs = []
+    inner = planes - 2
+    for y, span in ((y_low, slice(0, G)), (y_high, slice(rows - G, rows))):
+        for d in range(EARLY, 7):
+            at = inner * (d - EARLY)
+            pairs.append((coefs.at[d, 1 : planes - 1, span], y.at[at : at + inner]))
+        for d in range(6):
+            at = (7 - EARLY) * inner + planes * d
+            pairs.append((coefs.at[7 + d, :, span], y.at[at : at + planes]))
     run_copies(pairs, sems)
 
 
 def load_kernel(rhs, coefs, after, field, own, sems):
     planes, rows = rhs.shape[0], rhs.shape[1]
-    pairs = [(rhs, field.at[2 : planes + 2, G : rows + G])]
+    pairs = [(rhs, field.at[:, G : rows + G])]
     for p in range(planes):
         pairs.append((coefs.at[:, p], own.at[:, rows * p : rows * p + rows]))
     run_copies(pairs, sems)
 
 
-def relay_kernel(x_below, x_above, after, y_low, y_high):
-    rows = x_below.shape[1]
-    for n, x in enumerate((x_below, x_above)):
-        y_low[n] = x[:, 0:G]
-        y_high[n] = x[:, rows - G : rows]
-
-
 def tile_at(row):
     return pl.ds(pl.multiple_of(row, 8), 8)
 
 
-class Coefficients:
-    def __init__(self, rows, own, y_below, y_above, corners=None):
-        self.own, self.y_below, self.y_above, self.corners = own, y_below, y_above, corners
-        self.rows, self.tiles = rows, rows // 8 + 2
-
-    def spai(self, d, q, t):
-        return self.plane(d, q, t)
-
-    def oper(self, d, p, t):
-        return self.plane(7 + d, p, t)
-
-    def plane(self, d, p, t):
-        if t == 0:
-            return self.y_below[1 + d, tile_at(G * p), :]
-        if t == self.tiles - 1:
-            return self.y_above[1 + d, tile_at(G * p), :]
-        return self.own[d, tile_at(self.rows * p + 8 * t - 8), :]
-
-    def ghost(self, d, side, t):
-        x, c_below, c_above = self.corners[side]
-        if t == 0:
-            return c_below[side, 2 + d]
-        if t == self.tiles - 1:
-            return c_above[side, 2 + d]
-        return x[2 + d, 8 * t - 8 : 8 * t, :]
+def ghosted(t, tiles, below, middle, above):
+    if t == 0:
+        return below()
+    if t == tiles - 1:
+        return above()
+    return middle(8 * t - 8)
 
 
 def edges():
@@ -131,7 +120,7 @@
     return value
 
 
-def stencil(field, at, emit):
+def stencil(field, at, emit, skip=None, only=None):
     tiles = field.shape[1] // 8
     lanes = field.shape[2]
     row = lax.broadcasted_iota(jnp.int32, (8, lanes), 0)
@@ -143,41 +132,93 @@
         value = field[at, 8 * t : 8 * t + 8, :]
         return value, pltpu.roll(value, 1, 0), pltpu.roll(value, 7, 0)
 
+    if only == "ghosts":
+        ends = tile(tiles - 2), tile(tiles - 1)
     before = here = tile(0)
     for t in range(tiles):
+        if only == "ghosts" and 0 < t < tiles - 1:
+            before, here = ends
+            continue
         after = tile(t + 1) if t + 1 < tiles else here
         value = here[0]
         span = slice(8 * t, 8 * t + 8)
-        near = (
-            field[at - 1, span, :],
-            field[at + 1, span, :],
+        near = [
+            None if skip == 0 else field[at - 1, span, :],
+            None if skip == 1 else field[at + 1, span, :],
             jnp.where(top, before[1], here[1]),
             jnp.where(bottom, after[2], here[2]),
             jnp.where(left, 0.0, pltpu.roll(value, 1, 1)),
             jnp.where(right, 0.0, pltpu.roll(value, lanes - 1, 1)),
-        )
-        emit(t, span, value, near)
+        ]
+        if only != "own" or 0 < t < tiles - 1:
+            emit(t, span, value, near)
         before, here = here, after
 
 
-def spai_plane(edge, coefficient, field, image, q):
+def spai_plane(edge, coefficient, field, at, store, skip=None, only=None):
+    tiles = field.shape[1] // 8
+
     def emit(t, span, value, near):
         total = coefficient(0, t) * value
         for d in range(6):
-            total = total + coefficient(1 + d, t) * near[d]
-        image[q + 1, span, :] = within(edge, t, image.shape[1] // 8, total)
-
-    stencil(field, q + 2, emit)
-
-
-def oper_plane(edge, shift, coefs, field, image, out, p):
+            if near[d] is not None:
+                total = total + coefficient(1 + d, t) * near[d]
+        store(span, within(edge, t, tiles, total))
+
+    stencil(field, at, emit, skip, only)
+
+
+def face_coefficient(side, planes, tiles, middle, y_below, y_above):
+    at = planes + 7 * side
+    return lambda d, t: ghosted(t, tiles, lambda: y_below[at + d], lambda r: middle(d, r), lambda: y_above[at + d])
+
+
+def face_kernel(field, own, y_below, y_above, x_low, x_high, hold):
+    edge = edges()
+    planes, tall = field.shape[0], field.shape[1]
+    rows, tiles = tall - 2 * G, tall // 8
+    for n, p in enumerate((0, 1, planes - 2, planes - 1)):
+        hold[n, 0:G, :] = y_below[p] * edge[0]
+        hold[n, G : tall - G, :] = field[p, G : tall - G, :]
+        hold[n, tall - G : tall, :] = y_above[p] * edge[1]
+    for side, (x, at, p) in enumerate(((x_low, 0, 0), (x_high, 3, planes - 1))):
+        coefficient = face_coefficient(
+            side, planes, tiles, lambda d, r: own[d, rows * p + r : rows * p + r + 8, :], y_below, y_above
+        )
+
+        def store(span, value):
+            x[0, span, :] = value
+
+        spai_plane(edge, coefficient, hold, at, store, skip=side)
+        x[1] = hold[at]
+        for t in range(tiles):
+            x[2, 8 * t : 8 * t + 8, :] = coefficient(1 + side, t)
+
+
+def oper_coefficient(planes, rows, tiles, own, z_below, z_above, p):
+    def coefficient(d, t):
+        at = (7 - EARLY) * (planes - 2) + planes * d + p
+        return ghosted(
+            t, tiles, lambda: z_below[at], lambda r: own[7 + d, tile_at(rows * p + r), :], lambda: z_above[at]
+        )
+
+    return coefficient
+
+
+def oper_plane(edge, shift, own, z_below, z_above, field, image, out, p, skip=None):
+    planes, tiles = field.shape[0], field.shape[1] // 8
+    rows = field.shape[1] - 2 * G
+
+    coefficient = oper_coefficient(planes, rows, tiles, own, z_below, z_above, p)
+
     def emit(t, span, value, near):
-        total = value - shift * field[p + 2, span, :]
+        total = value - shift * field[p, span, :]
         for d in range(6):
-            total = total - coefs.oper(d, p, t) * near[d]
-        out[p + 2, span, :] = within(edge, t, out.shape[1] // 8, GROWTH * total)
-
-    stencil(image, p + 1, emit)
+            if near[d] is not None:
+                total = total - coefficient(d, t) * near[d]
+        out[p, span, :] = within(edge, t, tiles, GROWTH * total)
+
+    stencil(image, p + 1, emit, skip)
 
 
 def each(first, count, jump, work):
@@ -190,61 +231,84 @@
     lax.fori_loop(0, count, one, 0)
 
 
-def inner_work(shift, edge, coefs, field, image, out):
-    planes = image.shape[0] - 2
-    each(1, planes - 2, 0, lambda q: spai_plane(edge, lambda d, t: coefs.spai(d, q, t), field, image, q))
-    each(2, planes - 4, 0, lambda p: oper_plane(edge, shift, coefs, field, image, out, p))
-
-
-def outer_work(shift, edge, coefs, field, image, out):
-    planes = image.shape[0] - 2
-    for side, q in enumerate((-1, planes)):
-        spai_plane(edge, lambda d, t: coefs.ghost(d, side, t), field, image, q)
-    each(0, 2, planes - 2, lambda q: spai_plane(edge, lambda d, t: coefs.spai(d, q, t), field, image, q))
-    each(0, 4, planes - 4, lambda p: oper_plane(edge, shift, coefs, field, image, out, p))
-
-
-def send_edges(out, x_low, x_high):
-    planes = out.shape[0] - 4
-    x_low[...] = out[2:4]
-    x_high[...] = out[planes : planes + 2]
-
-
-def first_inner_kernel(shifts, own, y_below, y_above, field0, field, image, out):
+def image_planes(edge, own, z_below, z_above, y_below, y_above, field, image, only=None):
+    planes, tiles = field.shape[0], field.shape[1] // 8
+    rows = field.shape[1] - 2 * G
+
+    def image_plane(p):
+        def coefficient(d, t):
+            if only == "own":
+                return own[d, tile_at(rows * p + 8 * t - 8), :]
+            ghosts = (y_below, y_above) if d < EARLY else (z_below, z_above)
+            at = planes + 14 + (planes - 2) * d if d < EARLY else (planes - 2) * (d - EARLY)
+            below, above = (ghost.at[at + p - 1] for ghost in ghosts)
+            return ghosted(t, tiles, lambda: below[...], lambda r: own[d, tile_at(rows * p + r), :], lambda: above[...])
+
+        def store(span, value):
+            image[p + 1, span, :] = value
+
+        spai_plane(edge, coefficient, field, p, store, None, only)
+
+    each(1, planes - 2, 0, image_plane)
+
+
+def inner_work(shift, edge, own, z_below, z_above, y_below, y_above, field, image, out, only=None):
+    planes = field.shape[0]
+    image_planes(edge, own, z_below, z_above, y_below, y_above, field, image, only)
+    each(2, planes - 4, 0, lambda p: oper_plane(edge, shift, own, z_below, z_above, field, image, out, p))
+    for skip, p in ((0, 1), (1, planes - 2)):
+        oper_plane(edge, shift, own, z_below, z_above, field, image, out, p, skip)
+
+
+def first_own_kernel(own, y_below, y_above, field0, field, image):
     edge = edges()
-    planes, tall = image.shape[0] - 2, image.shape[1]
-    for p in range(planes):
-        field[p + 2, 0:G, :] = y_below[0, G * p : G * p + G, :] * edge[0]
-        field[p + 2, tall - G : tall, :] = y_above[0, G * p : G * p + G, :] * edge[1]
-    inner_work(shifts[0], edge, Coefficients(field.shape[1] - 2 * G, own, y_below, y_above), field, image, out)
-
-
-def inner_kernel(step, shifts, own, y_below, y_above, field, image, out):
-    inner_work(shifts[step], edges(), Coefficients(field.shape[1] - 2 * G, own, y_below, y_above), field, image, out)
-
-
-def outer_kernel(step, shifts, own, y_below, y_above, x_below, x_above, c_below, c_above, *refs):
+    planes, tall = field.shape[0], field.shape[1]
+    field[:, 0:G, :] = y_below[0:planes] * edge[0]
+    field[:, tall - G : tall, :] = y_above[0:planes] * edge[1]
+    image_planes(edge, own, None, None, y_below, y_above, field, image, "own")
+
+
+def first_inner_kernel(shifts, own, z_below, z_above, y_below, y_above, field, image0, image, out):
+    inner_work(shifts[0], edges(), own, z_below, z_above, y_below, y_above, field, image, out, "ghosts")
+
+
+def inner_kernel(step, shifts, own, z_below, z_above, y_below, y_above, field, image, out):
+    inner_work(shifts[step], edges(), own, z_below, z_above, y_below, y_above, field, image, out)
+
+
+def outer_kernel(step, shifts, own, z_below, z_above, y_below, y_above, far_low, far_high, my_low, my_high, *refs):
+    if step == 0:
+        low, high, below, above = my_low, my_high, far_low, far_high
+    else:
+        low, high, below, above, *refs = refs
+    if step == 3:
+        refs = refs[1:]
+    field, image0, out0, image, out, *sends = refs
     edge = edges()
-    first = step == 0
-    if first:
-        field0, image0, out0, field, image, out, *sends = refs
-    else:
-        if step == 3:
-            refs = refs[1:]
-        v_below, v_above, field0, image0, out0, field, image, out, *sends = refs
-    planes, tall = image.shape[0] - 2, image.shape[1]
-    if first:
-        for side, (x, at) in enumerate(((x_below, 0), (x_above, planes + 2))):
-            field[at : at + 2, 0:G, :] = c_below[side, 0:2] * edge[0]
-            field[at : at + 2, G : tall - G, :] = x[0:2]
-            field[at : at + 2, tall - G : tall, :] = c_above[side, 0:2] * edge[1]
-    else:
-        field[0:2] = v_below[...]
-        field[planes + 2 : planes + 4] = v_above[...]
-    corners = ((x_below, c_below, c_above), (x_above, c_below, c_above))
-    outer_work(shifts[step], edge, Coefficients(field.shape[1] - 2 * G, own, y_below, y_above, corners), field, image, out)
-    if sends:
-        send_edges(out, *sends)
+    planes, tall = field.shape[0], field.shape[1]
+    rows, tiles = tall - 2 * G, tall // 8
+    for t in range(tiles):
+        span = slice(8 * t, 8 * t + 8)
+        image[0, span, :] = below[0, span, :] + far_low[2, span, :] * field[0, span, :]
+        image[1, span, :] = low[0, span, :] + my_low[2, span, :] * below[1, span, :]
+        image[planes, span, :] = high[0, span, :] + my_high[2, span, :] * above[1, span, :]
+        image[planes + 1, span, :] = above[0, span, :] + far_high[2, span, :] * field[planes - 1, span, :]
+    for skip, p, face in ((0, 1, 1), (1, planes - 2, planes)):
+        coefficient = oper_coefficient(planes, rows, tiles, own, z_below, z_above, p)
+        for t in range(tiles):
+            span = slice(8 * t, 8 * t + 8)
+            out[p, span, :] = out[p, span, :] - GROWTH * (coefficient(skip, t) * image[face, span, :])
+    each(0, 2, planes - 2, lambda p: oper_plane(edge, shifts[step], own, z_below, z_above, field, image, out, p))
+    for side, (x, at) in enumerate(zip(sends, (0, planes - 1))):
+        coefficient = face_coefficient(
+            side, planes, tiles, lambda d, r: own[d, rows * at + r : rows * at + r + 8, :], y_below, y_above
+        )
+
+        def store(span, value):
+            x[0, span, :] = value
+
+        spai_plane(edge, coefficient, out, at, store, skip=side)
+        x[1] = out[at]
 
 
 def pair_rows(count):
@@ -252,13 +316,13 @@
 
 
 def gram_rows(fields, pairs, out, start):
-    planes = fields[0].shape[0] - 4
+    planes = fields[0].shape[0]
     rows = fields[0].shape[1] - 2 * G
 
     def one(p, sums):
         sums = list(sums)
         for r in range(G, rows + G, 8):
-            values = [f[p + 2, r : r + 8, :] for f in fields]
+            values = [f[p, r : r + 8, :] for f in fields]
             for k, (i, j) in enumerate(pairs):
                 sums[k] = sums[k] + values[i] * values[j]
         return tuple(sums)
@@ -376,25 +440,29 @@
         triples = ((made.at[0:5, p], basis.at[:, p]), (made.at[5, p], solution_out.at[p]), (made.at[6, p], residual_out.at[p]))
         return [pltpu.make_async_copy(source, target, sems.at[p, n]) for n, (source, target) in enumerate(triples)]
 
+    def blocks():
+        return [(r, c) for r in range(0, made.shape[2], 8) for c in range(0, made.shape[3], 128)]
+
     def one(p, carry):
-        for r in range(0, made.shape[2], 8):
-            for c in range(0, made.shape[3], 128):
-                v = [f[p + 2, r + G : r + G + 8, c : c + 128] for f in fields]
-                w = [f[p + 1, r + G : r + G + 8, c : c + 128] for f in images]
-                for k in range(5):
-                    total = inverse[0][k] * v[0]
-                    for j in range(1, k + 1):
-                        total = total + inverse[j][k] * v[j]
-                    made[k, p, r : r + 8, c : c + 128] = total
-                total = weights[0] * w[0]
-                for k in range(1, 4):
-                    total = total + weights[k] * w[k]
-                made[5, p, r : r + 8, c : c + 128] = total
-                total = combine[0] * v[0]
-                for j in range(1, 5):
-                    total = total + combine[j] * v[j]
-                made[6, p, r : r + 8, c : c + 128] = total
-        for copy in copies(p):
+        for r, c in blocks():
+            v = [f[p, r + G : r + G + 8, c : c + 128] for f in fields]
+            for k in range(5):
+                total = inverse[0][k] * v[0]
+                for j in range(1, k + 1):
+                    total = total + inverse[j][k] * v[j]
+                made[k, p, r : r + 8, c : c + 128] = total
+        first, *others = copies(p)
+        first.start()
+        for r, c in blocks():
+            total = weights[0] * images[0][p + 1, r + G : r + G + 8, c : c + 128]
+            for k in range(1, 4):
+                total = total + weights[k] * images[k][p + 1, r + G : r + G + 8, c : c + 128]
+            made[5, p, r : r + 8, c : c + 128] = total
+            total = combine[0] * fields[0][p, r + G : r + G + 8, c : c + 128]
+            for j in range(1, 5):
+                total = total + combine[j] * fields[j][p, r + G : r + G + 8, c : c + 128]
+            made[6, p, r : r + 8, c : c + 128] = total
+        for copy in others:
             copy.start()
         return carry
 
@@ -419,48 +487,61 @@
 def body(rhs, coefs, shifts):
     planes, rows, lanes = rhs.shape
     tall = rows + 2 * G
-    field = on_chip(planes + 4, tall, lanes)
+    field = on_chip(planes, tall, lanes)
     image = on_chip(planes + 2, tall, lanes)
-    halo = on_chip(2, tall, lanes)
-    x_cut, y_cut = on_chip(9, rows, lanes), on_chip(14, G * planes, lanes)
-    corner = on_chip(2, 9, G, lanes)
-    x_low, x_high, y_low, y_high = call(
-        cut_kernel, "cut", [rhs, coefs], [ANY] * 2, [x_cut, x_cut, y_cut, y_cut],
-        scratch=[pltpu.SemaphoreType.DMA((4 + 4 * planes,))],
+    first_face, face = on_chip(3, tall, lanes), on_chip(2, tall, lanes)
+    y_cut = on_chip(planes + 14 + EARLY * (planes - 2), G, lanes)
+    z_cut = on_chip((7 - EARLY) * (planes - 2) + 6 * planes, G, lanes)
+    y_low, y_high = call(
+        cut_rows_kernel, "cut_rows", [rhs, coefs], [ANY] * 2, [y_cut, y_cut], scratch=[pltpu.SemaphoreType.DMA((6 + 2 * EARLY,))]
     )
-    x_below, x_above = both_ways(x_low, x_high, GX)
     y_below, y_above = both_ways(y_low, y_high, "gy")
+    z_low, z_high = call(
+        cut_rest_kernel, "cut_rest", [coefs, y_low], [ANY, VM], [z_cut, z_cut],
+        scratch=[pltpu.SemaphoreType.DMA((2 * (13 - EARLY),))],
+    )
+    z_below, z_above = both_ways(z_low, z_high, "gy")
     v, own = call(
-        load_kernel, "load", [rhs, coefs, y_low], [ANY, ANY, VM], [field, on_chip(13, planes * rows, lanes)],
+        load_kernel, "load", [rhs, coefs, z_low], [ANY, ANY, VM], [field, on_chip(13, planes * rows, lanes)],
         scratch=[pltpu.SemaphoreType.DMA((1 + planes,))],
     )
-    c_low, c_high = call(relay_kernel, "relay", [x_below, x_above, own], [VM] * 3, [corner, corner])
-    c_below, c_above = both_ways(c_low, c_high, "gy")
+    my_low, my_high = call(
+        face_kernel, "face", [v, own, y_below, y_above], [VM] * 4, [first_face, first_face],
+        scratch=[pltpu.VMEM((4, tall, lanes), F32)],
+    )
+    far_low, far_high = both_ways(my_low, my_high, GX)
     basis, images = [], []
+    low = high = below = above = None
     for step in range(4):
-        common = [shifts, own, y_below, y_above]
-        specs = [SM] + [VM] * 3
+        common = [shifts, own, z_below, z_above]
         if step == 0:
-            v, w, out = call(
-                first_inner_kernel, "first_inner", common + [v], specs + [VM], [field, image, field], aliases={4: 0}
+            v, w = call(
+                first_own_kernel, "first_own", [own, y_below, y_above, v], [VM] * 4, [field, image], aliases={3: 0}
+            )
+            w, out = call(
+                first_inner_kernel, "first_inner", common + [y_below, y_above, v, w], [SM] + [VM] * 7,
+                [image, field], aliases={7: 0},
             )
         else:
-            w, out = call(functools.partial(inner_kernel, step), "inner", common + [v], specs + [VM], [image, field])
-        common += [x_below, x_above, c_below, c_above]
+            w, out = call(
+                functools.partial(inner_kernel, step), "inner", common + [y_below, y_above, v], [SM] + [VM] * 6, [image, field]
+            )
+        common += [y_below, y_above, far_low, far_high, my_low, my_high]
+        if step > 0:
+            common += [low, high, below, above]
         if step == 3:
             (early,) = call(early_gram_kernel, "early_gram", basis + [v], [VM] * 4, [on_chip(16, 128)])
             common += [early]
-        common += [] if step == 0 else [below, above]
-        specs += [VM] * (len(common) - 4)
+        common += [v]
         at = len(common)
-        v, w, out, *sends = call(
-            functools.partial(outer_kernel, step),
-            "first_outer" if step == 0 else "outer",
-            common + [v, w, out], specs + [VM] * 3,
-            [field, image, field] + [halo, halo] * (step < 3), aliases={at: 0, at + 1: 1, at + 2: 2},
+        w, out, *sends = call(
+            functools.partial(outer_kernel, step), "first_outer" if step == 0 else "outer",
+            common + [w, out], [SM] + [VM] * (at + 1), [image, field] + [face, face] * (step < 3),
+            aliases={at: 0, at + 1: 1},
         )
         if sends:
-            below, above = both_ways(*sends, GX)
+            low, high = sends
+            below, above = both_ways(low, high, GX)
         basis.append(v)
         images.append(w)
         v = out

time: 88.8 us -> 85.6 us (0.964)
  starting transfers between devices: 23.3 us -> 28.7 us
  waiting for transfers between devices: 14.5 us -> 10.1 us
  blocking collectives: 27.5 us -> 23.3 us
    ppermute x6, waiting for transfers between devices: 8.15 us -> 2.7 us  [both_ways(): lax.ppermute(low, axis, ring(count, -1))]
    ppermute x6, starting transfers between devices: 14.2 us -> 19.5 us  [both_ways(): lax.ppermute(low, axis, ring(count, -1))]
    all_to_all x1, blocking collectives: 27.5 us -> 23.3 us  [body(): lines = lax.all_to_all(line, EVERY, 0, 0, tiled=True)]
    ppermute x6, waiting for transfers between devices: 6.37 us -> 7.4 us  [both_ways(): lax.ppermute(high, axis, ring(count, 1))]
    pallas_call x14 -> x16, Pallas kernels: 22.5 us -> 22.4 us  [call(): pl.pallas_call(kernel, name=name, out_shape=outs, in_specs=specs, out_spe...]
  transfers between devices with their start and end apart: 12 -> 12, of which waited for: 7 -> 6; matrix products, arithmetic and copies ran while one was open for 0% -> 0% of each run, Pallas kernels for 12% -> 16%
where the time goes in v2:
time: 85.6 us; the launch traced here: 85.3 us
  starting transfers between devices  28.7 us (34%)
  blocking collectives  23.3 us (27%)
  Pallas kernels  22.4 us (26%)
  waiting for transfers between devices  10.1 us (12%)
    all_to_all x1, blocking collectives, body(): lines = lax.all_to_all(line, EVERY, 0, 0, tiled=True)  23.3 us
    pallas_call x16, Pallas kernels, call(): pl.pallas_call(kernel, name=name, out_shape=outs, in_specs=specs, out_spe...  22.4 us
    ppermute x6, starting transfers between devices, both_ways(): lax.ppermute(low, axis, ring(count, -1))  19.5 us
    ppermute x6, starting transfers between devices, both_ways(): lax.ppermute(high, axis, ring(count, 1))  9.2 us
    ppermute x6, waiting for transfers between devices, both_ways(): lax.ppermute(high, axis, ring(count, 1))  7.4 us
    ppermute x6, waiting for transfers between devices, both_ways(): lax.ppermute(low, axis, ring(count, -1))  2.7 us
  transfers between devices with their start and end apart: 12, of which 6 were waited for; matrix products, arithmetic and copies ran while one was open for 0% of the time, Pallas kernels for 16%

profile of v2, /device:TPU:1, one launch (start us, length us, event | category | flops | bytes accessed | tf_op | source)
XLA Modules:
  0.0 85.3 jit_solution(1374192791055865820)
XLA Ops:
  0.6 1.2 %cut_rows.1 = (f32[46,8,256]{2,1,0:T(8,128)S(1)}, f32[46,8,256]{2,1,0:T(8,128)S(1)}) custom-call(f32[8,64,256]{2,1,0:T(8,128)} %rhs.3, f32[13,8,64,256]{3,2,1,0:T(8,128)} %coefs.5), custom_call_target="tpu_custom_call" | custom-call | tf_op jit(solution)/shard_map/cut_rows/pallas_call | solution.py:36
  1.9 2.1 %collective-permute-start = (f32[46,8,256]{2,1,0:T(8,128)S(1)}, f32[46,8,256]{2,1,0:T(8,128)S(1)}, u32[]{:S(2)}, u32[]{:S(2)}) collective-permute-start(f32[46,8,256]{2,1,0:T(8,128)S(1)} %get-tuple-element.39), channel_id=1, source_target_pairs={{0,1},{1,2},{2,3},{3,0},{4,5},{5,6},{6,7},{7,4},{8,9},{9,10},{10,1... | collective-permute-start | bytes 1130504 | tf_op jit(solution)/shard_map/ppermute | solution.py:484
  4.0 1.4 %collective-permute-start.1 = (f32[46,8,256]{2,1,0:T(8,128)S(1)}, f32[46,8,256]{2,1,0:T(8,128)S(1)}, u32[]{:S(2)}, u32[]{:S(2)}) collective-permute-start(f32[46,8,256]{2,1,0:T(8,128)S(1)} %get-tuple-element.36.after), channel_id=1, source_target_pairs={{0,3},{1,0},{2,1},{3,2},{4,7},{5,4},{6,5},{7,6},{8,11},{9,8},{10,9... | collective-permute-start | bytes 1130504 | tf_op jit(solution)/shard_map/ppermute | solution.py:484
  5.4 1.4 %cut_rest.1 = (f32[66,8,256]{2,1,0:T(8,128)S(1)}, f32[66,8,256]{2,1,0:T(8,128)S(1)}) custom-call(f32[13,8,64,256]{3,2,1,0:T(8,128)} %coefs.5, f32[46,8,256]{2,1,0:T(8,128)S(1)} %get-tuple-element.36.after), custom_call_target="tpu_custom_call" | custom-call | tf_op jit(solution)/shard_map/cut_rest/pallas_call | solution.py:36
  6.8 0.2 collective-permute-start.2
  7.0 2.6 %collective-permute-start.3 = (f32[66,8,256]{2,1,0:T(8,128)S(1)}, f32[66,8,256]{2,1,0:T(8,128)S(1)}, u32[]{:S(2)}, u32[]{:S(2)}) collective-permute-start(f32[66,8,256]{2,1,0:T(8,128)S(1)} %get-tuple-element.37.after), channel_id=1, source_target_pairs={{0,3},{1,0},{2,1},{3,2},{4,7},{5,4},{6,5},{7,6},{8,11},{9,8},{10,9... | collective-permute-start | bytes 1622024 | tf_op jit(solution)/shard_map/ppermute | solution.py:484
  9.5 3.2 %load.1 = (f32[8,80,256]{2,1,0:T(8,128)S(1)}, f32[13,512,256]{2,1,0:T(8,128)S(1)}) custom-call(f32[8,64,256]{2,1,0:T(8,128)} %rhs.3, f32[13,8,64,256]{3,2,1,0:T(8,128)} %coefs.5, f32[66,8,256]{2,1,0:T(8,128)S(1)} %get-tuple-element.37.after), custom_call_target="tpu_custom_call" | custom-call | tf_op jit(solution)/shard_map/load/pallas_call | solution.py:36
  12.7 0.0 collective-permute-done.y_below
  12.7 0.2 collective-permute-done.1.y_above
  13.0 0.0 copy-start
  13.0 0.2 face.1
  13.1 5.3 %collective-permute-start.4 = (f32[3,80,256]{2,1,0:T(8,128)S(1)}, f32[3,80,256]{2,1,0:T(8,128)S(1)}, u32[]{:S(2)}, u32[]{:S(2)}) collective-permute-start(f32[3,80,256]{2,1,0:T(8,128)S(1)} %get-tuple-element.43.my_high), channel_id=1, source_target_pairs={{0,4},{4,8},{8,12},{12,16},{16,20},{20,24},{24,28},{28,32},{32,36}... | collective-permute-start | bytes 737288 | tf_op jit(solution)/shard_map/ppermute | solution.py:484
  18.4 0.0 collective-permute-start.5
  18.5 0.7 first_own.1
  19.2 3.9 %collective-permute-done.2.z_below = f32[66,8,256]{2,1,0:T(8,128)S(1)} collective-permute-done((f32[66,8,256]{2,1,0:T(8,128)S(1)}, f32[66,8,256]{2,1,0:T(8,128)S(1)}, u32[]{:S(2)}, u32[]{:S(2)}) %collective-permute-start.2) | collective-permute-done | bytes 540704 | tf_op jit(solution)/shard_map/ppermute | solution.py:484
  23.0 1.5 %collective-permute-done.3.z_above = f32[66,8,256]{2,1,0:T(8,128)S(1)} collective-permute-done((f32[66,8,256]{2,1,0:T(8,128)S(1)}, f32[66,8,256]{2,1,0:T(8,128)S(1)}, u32[]{:S(2)}, u32[]{:S(2)}) %collective-permute-start.3) | collective-permute-done | bytes 540704 | tf_op jit(solution)/shard_map/ppermute | solution.py:484
  24.5 0.0 copy-done
  24.6 1.7 %first_inner.1 = (f32[10,80,256]{2,1,0:T(8,128)S(1)}, f32[8,80,256]{2,1,0:T(8,128)S(1)}) custom-call(f32[4]{0:T(128)S(1)} %copy-done, f32[13,512,256]{2,1,0:T(8,128)S(1)} %get-tuple-element.38.own, f32[66,8,256]{2,1,0:T(8,128)S(1)} %collective-permute-done.2.z_below, ...), custom_call_target="tpu_custom_call", output_to_operand_aliasing={{0}: (7, {})} | custom-call | tf_op jit(solution)/shard_map/first_inner/pallas_call | solution.py:36
  26.2 0.0 collective-permute-done.4.far_low
  26.3 0.0 collective-permute-done.5.far_high
  26.3 1.0 %first_outer.1 = (f32[10,80,256]{2,1,0:T(8,128)S(1)}, f32[8,80,256]{2,1,0:T(8,128)S(1)}, f32[2,80,256]{2,1,0:T(8,128)S(1)}, f32[2,80,256]{2,1,0:T(8,128)S(1)}) custom-call(f32[4]{0:T(128)S(1)} %copy-done, f32[13,512,256]{2,1,0:T(8,128)S(1)} %get-tuple-element.38.own, ...), custom_call_target="tpu_custom_call", output_to_operand_aliasing={{0}: (11, {}), {1}: (12, {})} | custom-call | tf_op jit(solution)/shard_map/first_outer/pallas_call | solution.py:36
  27.3 2.3 %collective-permute-start.7 = (f32[2,80,256]{2,1,0:T(8,128)S(1)}, f32[2,80,256]{2,1,0:T(8,128)S(1)}, u32[]{:S(2)}, u32[]{:S(2)}) collective-permute-start(f32[2,80,256]{2,1,0:T(8,128)S(1)} %get-tuple-element.49.refs_0_), channel_id=1, source_target_pairs={{0,252},{4,0},{8,4},{12,8},{16,12},{20,16},{24,20},{28,24},{32,28}... | collective-permute-start | bytes 491528 | tf_op jit(solution)/shard_map/ppermute | solution.py:484
  29.6 1.6 %collective-permute-start.6 = (f32[2,80,256]{2,1,0:T(8,128)S(1)}, f32[2,80,256]{2,1,0:T(8,128)S(1)}, u32[]{:S(2)}, u32[]{:S(2)}) collective-permute-start(f32[2,80,256]{2,1,0:T(8,128)S(1)} %get-tuple-element.50.refs_1_), channel_id=1, source_target_pairs={{0,4},{4,8},{8,12},{12,16},{16,20},{20,24},{24,28},{28,32},{32,36}... | collective-permute-start | bytes 491528 | tf_op jit(solution)/shard_map/ppermute | solution.py:484
  31.2 2.0 %inner.3 = (f32[10,80,256]{2,1,0:T(8,128)S(1)}, f32[8,80,256]{2,1,0:T(8,128)S(1)}) custom-call(f32[4]{0:T(128)S(1)} %copy-done, f32[13,512,256]{2,1,0:T(8,128)S(1)} %get-tuple-element.38.own, f32[66,8,256]{2,1,0:T(8,128)S(1)} %collective-permute-done.2.z_below, f32[66,8,256]{2,1,0:T(8,128)S(1)} %collective-permute-done.3.z_above, ...), custom_call_target="tpu_custom_call" | custom-call | tf_op jit(solution)/shard_map/inner/pallas_call | solution.py:36
  33.2 1.0 %collective-permute-done.7.refs_3_ = f32[2,80,256]{2,1,0:T(8,128)S(1)} collective-permute-done((f32[2,80,256]{2,1,0:T(8,128)S(1)}, f32[2,80,256]{2,1,0:T(8,128)S(1)}, u32[]{:S(2)}, u32[]{:S(2)}) %collective-permute-start.7) | collective-permute-done | bytes 163872 | tf_op jit(solution)/shard_map/ppermute | solution.py:484
  34.1 3.2 %collective-permute-done.6.refs_2_ = f32[2,80,256]{2,1,0:T(8,128)S(1)} collective-permute-done((f32[2,80,256]{2,1,0:T(8,128)S(1)}, f32[2,80,256]{2,1,0:T(8,128)S(1)}, u32[]{:S(2)}, u32[]{:S(2)}) %collective-permute-start.6) | collective-permute-done | bytes 163872 | tf_op jit(solution)/shard_map/ppermute | solution.py:484
  37.4 1.0 %outer.3 = (f32[10,80,256]{2,1,0:T(8,128)S(1)}, f32[8,80,256]{2,1,0:T(8,128)S(1)}, f32[2,80,256]{2,1,0:T(8,128)S(1)}, f32[2,80,256]{2,1,0:T(8,128)S(1)}) custom-call(f32[4]{0:T(128)S(1)} %copy-done, f32[13,512,256]{2,1,0:T(8,128)S(1)} %get-tuple-element.38.own, ...), custom_call_target="tpu_custom_call", output_to_operand_aliasing={{0}: (15, {}), {1}: (16, {})} | custom-call | tf_op jit(solution)/shard_map/outer/pallas_call | solution.py:36
  38.4 7.3 %collective-permute-start.9 = (f32[2,80,256]{2,1,0:T(8,128)S(1)}, f32[2,80,256]{2,1,0:T(8,128)S(1)}, u32[]{:S(2)}, u32[]{:S(2)}) collective-permute-start(f32[2,80,256]{2,1,0:T(8,128)S(1)} %get-tuple-element.54.refs_0_), channel_id=1, source_target_pairs={{0,252},{4,0},{8,4},{12,8},{16,12},{20,16},{24,20},{28,24},{32,28}... | collective-permute-start | bytes 491528 | tf_op jit(solution)/shard_map/ppermute | solution.py:484
  45.7 0.0 collective-permute-start.8
  45.7 1.9 %inner.4 = (f32[10,80,256]{2,1,0:T(8,128)S(1)}, f32[8,80,256]{2,1,0:T(8,128)S(1)}) custom-call(f32[4]{0:T(128)S(1)} %copy-done, f32[13,512,256]{2,1,0:T(8,128)S(1)} %get-tuple-element.38.own, f32[66,8,256]{2,1,0:T(8,128)S(1)} %collective-permute-done.2.z_below, f32[66,8,256]{2,1,0:T(8,128)S(1)} %collective-permute-done.3.z_above, ...), custom_call_target="tpu_custom_call" | custom-call | tf_op jit(solution)/shard_map/inner/pallas_call | solution.py:36
  47.6 0.0 collective-permute-done.9.refs_3_
  47.6 0.3 collective-permute-done.8.refs_2_
  47.9 1.0 %outer.4 = (f32[10,80,256]{2,1,0:T(8,128)S(1)}, f32[8,80,256]{2,1,0:T(8,128)S(1)}, f32[2,80,256]{2,1,0:T(8,128)S(1)}, f32[2,80,256]{2,1,0:T(8,128)S(1)}) custom-call(f32[4]{0:T(128)S(1)} %copy-done, f32[13,512,256]{2,1,0:T(8,128)S(1)} %get-tuple-element.38.own, ...), custom_call_target="tpu_custom_call", output_to_operand_aliasing={{0}: (15, {}), {1}: (16, {})} | custom-call | tf_op jit(solution)/shard_map/outer/pallas_call | solution.py:36
  49.0 6.0 %collective-permute-start.11 = (f32[2,80,256]{2,1,0:T(8,128)S(1)}, f32[2,80,256]{2,1,0:T(8,128)S(1)}, u32[]{:S(2)}, u32[]{:S(2)}) collective-permute-start(f32[2,80,256]{2,1,0:T(8,128)S(1)} %get-tuple-element.59.refs_0_), channel_id=1, source_target_pairs={{0,252},{4,0},{8,4},{12,8},{16,12},{20,16},{24,20},{28,24},{32,28}... | collective-permute-start | bytes 491528 | tf_op jit(solution)/shard_map/ppermute | solution.py:484
  54.9 0.0 collective-permute-start.10
  54.9 0.4 early_gram.1.refs_4_.early
  55.3 1.9 %inner.5 = (f32[10,80,256]{2,1,0:T(8,128)S(1)}, f32[8,80,256]{2,1,0:T(8,128)S(1)}) custom-call(f32[4]{0:T(128)S(1)} %copy-done, f32[13,512,256]{2,1,0:T(8,128)S(1)} %get-tuple-element.38.own, f32[66,8,256]{2,1,0:T(8,128)S(1)} %collective-permute-done.2.z_below, f32[66,8,256]{2,1,0:T(8,128)S(1)} %collective-permute-done.3.z_above, ...), custom_call_target="tpu_custom_call" | custom-call | tf_op jit(solution)/shard_map/inner/pallas_call | solution.py:36
  57.3 0.0 collective-permute-done.11.refs_3_
  57.3 0.0 collective-permute-done.10.refs_2_
  57.3 0.9 %outer.5 = (f32[10,80,256]{2,1,0:T(8,128)S(1)}, f32[8,80,256]{2,1,0:T(8,128)S(1)}) custom-call(f32[4]{0:T(128)S(1)} %copy-done, f32[13,512,256]{2,1,0:T(8,128)S(1)} %get-tuple-element.38.own, f32[66,8,256]{2,1,0:T(8,128)S(1)} %collective-permute-done.2.z_below, ...), custom_call_target="tpu_custom_call", output_to_operand_aliasing={{0}: (16, {}), {1}: (17, {})} | custom-call | tf_op jit(solution)/shard_map/outer/pallas_call | solution.py:36
  58.2 0.3 late_gram.1
  58.5 23.3 %all_to_all.11 = f32[256,1,128]{2,1,0:T(1,128)S(1)} all-to-all(f32[256,1,128]{2,1,0:T(1,128)S(1)} %bitcast.5), channel_id=1, replica_groups=mesh['gx_0'=4,'gx_1'=8,'gx_2'=2,'gy'=4] {'gx_0','gx_1','gx_2','gy'}, dimensions={0} | all-to-all | bytes 262144 | tf_op jit(solution)/shard_map/all_to_all | solution.py:554
  81.9 3.4 %final.1 = (f32[5,8,64,256]{3,2,1,0:T(8,128)}, f32[5,5]{1,0:T(8,128)}, f32[8,64,256]{2,1,0:T(8,128)}, f32[8,64,256]{2,1,0:T(8,128)}) custom-call(f32[4]{0:T(128)S(1)} %copy-done, f32[256,128]{1,0:T(8,128)S(1)} %bitcast.4, f32[8,80,256]{2,1,0:T(8,128)S(1)} %get-tuple-element.41.field.refs_0_.v0.refs_2_, ...), custom_call_target="tpu_custom_call" | custom-call | tf_op jit(solution)/shard_map/final/pallas_call | solution.py:36
Async XLA Ops:
  1.9 10.8 %collective-permute-start = (f32[46,8,256]{2,1,0:T(8,128)S(1)}, f32[46,8,256]{2,1,0:T(8,128)S(1)}, u32[]{:S(2)}, u32[]{:S(2)}) collective-permute-start(f32[46,8,256]{2,1,0:T(8,128)S(1)} %get-tuple-element.39), channel_id=1, source_target_pairs={{0,1},{1,2},{2,3},{3,0},{4,5},{5,6},{6,7},{7,4},{8,9},{9,10},{10,1... | collective-permute-start | bytes 1130504 | tf_op jit(solution)/shard_map/ppermute | solution.py:484
  4.0 9.0 %collective-permute-start.1 = (f32[46,8,256]{2,1,0:T(8,128)S(1)}, f32[46,8,256]{2,1,0:T(8,128)S(1)}, u32[]{:S(2)}, u32[]{:S(2)}) collective-permute-start(f32[46,8,256]{2,1,0:T(8,128)S(1)} %get-tuple-element.36.after), channel_id=1, source_target_pairs={{0,3},{1,0},{2,1},{3,2},{4,7},{5,4},{6,5},{7,6},{8,11},{9,8},{10,9... | collective-permute-start | bytes 1130504 | tf_op jit(solution)/shard_map/ppermute | solution.py:484
  6.8 16.3 %collective-permute-start.2 = (f32[66,8,256]{2,1,0:T(8,128)S(1)}, f32[66,8,256]{2,1,0:T(8,128)S(1)}, u32[]{:S(2)}, u32[]{:S(2)}) collective-permute-start(f32[66,8,256]{2,1,0:T(8,128)S(1)} %get-tuple-element.42), channel_id=1, source_target_pairs={{0,1},{1,2},{2,3},{3,0},{4,5},{5,6},{6,7},{7,4},{8,9},{9,10},{10,1... | collective-permute-start | bytes 1622024 | tf_op jit(solution)/shard_map/ppermute | solution.py:484
  7.0 17.6 %collective-permute-start.3 = (f32[66,8,256]{2,1,0:T(8,128)S(1)}, f32[66,8,256]{2,1,0:T(8,128)S(1)}, u32[]{:S(2)}, u32[]{:S(2)}) collective-permute-start(f32[66,8,256]{2,1,0:T(8,128)S(1)} %get-tuple-element.37.after), channel_id=1, source_target_pairs={{0,3},{1,0},{2,1},{3,2},{4,7},{5,4},{6,5},{7,6},{8,11},{9,8},{10,9... | collective-permute-start | bytes 1622024 | tf_op jit(solution)/shard_map/ppermute | solution.py:484
  13.0 11.6 %copy-start = (f32[4]{0:T(128)S(1)}, f32[4]{0:T(128)}, u32[]{:S(2)}) copy-start(f32[4]{0:T(128)} %refs_0_.1) | copy-start | bytes 52
  13.1 13.1 %collective-permute-start.4 = (f32[3,80,256]{2,1,0:T(8,128)S(1)}, f32[3,80,256]{2,1,0:T(8,128)S(1)}, u32[]{:S(2)}, u32[]{:S(2)}) collective-permute-start(f32[3,80,256]{2,1,0:T(8,128)S(1)} %get-tuple-element.43.my_high), channel_id=1, source_target_pairs={{0,4},{4,8},{8,12},{12,16},{16,20},{20,24},{24,28},{28,32},{32,36}... | collective-permute-start | bytes 737288 | tf_op jit(solution)/shard_map/ppermute | solution.py:484
  18.4 7.8 %collective-permute-start.5 = (f32[3,80,256]{2,1,0:T(8,128)S(1)}, f32[3,80,256]{2,1,0:T(8,128)S(1)}, u32[]{:S(2)}, u32[]{:S(2)}) collective-permute-start(f32[3,80,256]{2,1,0:T(8,128)S(1)} %get-tuple-element.44.my_low), channel_id=1, source_target_pairs={{0,252},{4,0},{8,4},{12,8},{16,12},{20,16},{24,20},{28,24},{32,28}... | collective-permute-start | bytes 737288 | tf_op jit(solution)/shard_map/ppermute | solution.py:484
  27.3 6.8 %collective-permute-start.7 = (f32[2,80,256]{2,1,0:T(8,128)S(1)}, f32[2,80,256]{2,1,0:T(8,128)S(1)}, u32[]{:S(2)}, u32[]{:S(2)}) collective-permute-start(f32[2,80,256]{2,1,0:T(8,128)S(1)} %get-tuple-element.49.refs_0_), channel_id=1, source_target_pairs={{0,252},{4,0},{8,4},{12,8},{16,12},{20,16},{24,20},{28,24},{32,28}... | collective-permute-start | bytes 491528 | tf_op jit(solution)/shard_map/ppermute | solution.py:484
  29.6 7.8 %collective-permute-start.6 = (f32[2,80,256]{2,1,0:T(8,128)S(1)}, f32[2,80,256]{2,1,0:T(8,128)S(1)}, u32[]{:S(2)}, u32[]{:S(2)}) collective-permute-start(f32[2,80,256]{2,1,0:T(8,128)S(1)} %get-tuple-element.50.refs_1_), channel_id=1, source_target_pairs={{0,4},{4,8},{8,12},{12,16},{16,20},{20,24},{24,28},{28,32},{32,36}... | collective-permute-start | bytes 491528 | tf_op jit(solution)/shard_map/ppermute | solution.py:484
  38.4 9.2 %collective-permute-start.9 = (f32[2,80,256]{2,1,0:T(8,128)S(1)}, f32[2,80,256]{2,1,0:T(8,128)S(1)}, u32[]{:S(2)}, u32[]{:S(2)}) collective-permute-start(f32[2,80,256]{2,1,0:T(8,128)S(1)} %get-tuple-element.54.refs_0_), channel_id=1, source_target_pairs={{0,252},{4,0},{8,4},{12,8},{16,12},{20,16},{24,20},{28,24},{32,28}... | collective-permute-start | bytes 491528 | tf_op jit(solution)/shard_map/ppermute | solution.py:484
  45.7 2.3 %collective-permute-start.8 = (f32[2,80,256]{2,1,0:T(8,128)S(1)}, f32[2,80,256]{2,1,0:T(8,128)S(1)}, u32[]{:S(2)}, u32[]{:S(2)}) collective-permute-start(f32[2,80,256]{2,1,0:T(8,128)S(1)} %get-tuple-element.55.refs_1_), channel_id=1, source_target_pairs={{0,4},{4,8},{8,12},{12,16},{16,20},{20,24},{24,28},{28,32},{32,36}... | collective-permute-start | bytes 491528 | tf_op jit(solution)/shard_map/ppermute | solution.py:484
  49.0 8.3 %collective-permute-start.11 = (f32[2,80,256]{2,1,0:T(8,128)S(1)}, f32[2,80,256]{2,1,0:T(8,128)S(1)}, u32[]{:S(2)}, u32[]{:S(2)}) collective-permute-start(f32[2,80,256]{2,1,0:T(8,128)S(1)} %get-tuple-element.59.refs_0_), channel_id=1, source_target_pairs={{0,252},{4,0},{8,4},{12,8},{16,12},{20,16},{24,20},{28,24},{32,28}... | collective-permute-start | bytes 491528 | tf_op jit(solution)/shard_map/ppermute | solution.py:484
  54.9 2.4 %collective-permute-start.10 = (f32[2,80,256]{2,1,0:T(8,128)S(1)}, f32[2,80,256]{2,1,0:T(8,128)S(1)}, u32[]{:S(2)}, u32[]{:S(2)}) collective-permute-start(f32[2,80,256]{2,1,0:T(8,128)S(1)} %get-tuple-element.60.refs_1_), channel_id=1, source_target_pairs={{0,4},{4,8},{8,12},{12,16},{16,20},{20,24},{24,28},{28,32},{32,36}... | collective-permute-start | bytes 491528 | tf_op jit(solution)/shard_map/ppermute | solution.py:484

commit v3 on v2

--- a/solution.py
+++ b/solution.py
@@ -56,7 +56,7 @@
         copy.wait()
 
 
-EARLY = 4
+EARLY = 6
 
 
 def cut_rows_kernel(rhs, coefs, y_low, y_high, sems):

time: 85.6 us -> 85.6 us (level)
    ppermute x6, waiting for transfers between devices: 2.7 us -> 4.17 us  [both_ways(): lax.ppermute(low, axis, ring(count, -1))]
    ppermute x6, waiting for transfers between devices: 7.4 us -> 6.23 us  [both_ways(): lax.ppermute(high, axis, ring(count, 1))]
    ppermute x6, starting transfers between devices: 9.2 us -> 8.27 us  [both_ways(): lax.ppermute(high, axis, ring(count, 1))]
  transfers between devices with their start and end apart: 12 -> 12, of which waited for: 6 -> 8; matrix products, arithmetic and copies ran while one was open for 0% -> 0% of each run, Pallas kernels for 16% -> 16%
where the time goes in v3:
time: 85.6 us; the launch traced here: 85.4 us
  starting transfers between devices  28.5 us (33%)
  blocking collectives  23.3 us (27%)
  Pallas kernels  22.4 us (26%)
  waiting for transfers between devices  10.4 us (12%)
    all_to_all x1, blocking collectives, body(): lines = lax.all_to_all(line, EVERY, 0, 0, tiled=True)  23.3 us
    pallas_call x16, Pallas kernels, call(): pl.pallas_call(kernel, name=name, out_shape=outs, in_specs=specs, out_spe...  22.4 us
    ppermute x6, starting transfers between devices, both_ways(): lax.ppermute(low, axis, ring(count, -1))  20.2 us
    ppermute x6, starting transfers between devices, both_ways(): lax.ppermute(high, axis, ring(count, 1))  8.27 us
    ppermute x6, waiting for transfers between devices, both_ways(): lax.ppermute(high, axis, ring(count, 1))  6.23 us
    ppermute x6, waiting for transfers between devices, both_ways(): lax.ppermute(low, axis, ring(count, -1))  4.17 us
  transfers between devices with their start and end apart: 12, of which 8 were waited for; matrix products, arithmetic and copies ran while one was open for 0% of the time, Pallas kernels for 16%

profile of v3, /device:TPU:1, one launch (start us, length us, event | category | flops | bytes accessed | tf_op | source)
XLA Modules:
  0.0 85.4 jit_solution(5275816274034594314)
XLA Ops:
  0.6 1.3 %cut_rows.1 = (f32[58,8,256]{2,1,0:T(8,128)S(1)}, f32[58,8,256]{2,1,0:T(8,128)S(1)}) custom-call(f32[8,64,256]{2,1,0:T(8,128)} %rhs.3, f32[13,8,64,256]{3,2,1,0:T(8,128)} %coefs.5), custom_call_target="tpu_custom_call" | custom-call | tf_op jit(solution)/shard_map/cut_rows/pallas_call | solution.py:36
  2.0 2.1 %collective-permute-start = (f32[58,8,256]{2,1,0:T(8,128)S(1)}, f32[58,8,256]{2,1,0:T(8,128)S(1)}, u32[]{:S(2)}, u32[]{:S(2)}) collective-permute-start(f32[58,8,256]{2,1,0:T(8,128)S(1)} %get-tuple-element.39), channel_id=1, source_target_pairs={{0,1},{1,2},{2,3},{3,0},{4,5},{5,6},{6,7},{7,4},{8,9},{9,10},{10,1... | collective-permute-start | bytes 1425416 | tf_op jit(solution)/shard_map/ppermute | solution.py:484
  4.1 1.4 %collective-permute-start.1 = (f32[58,8,256]{2,1,0:T(8,128)S(1)}, f32[58,8,256]{2,1,0:T(8,128)S(1)}, u32[]{:S(2)}, u32[]{:S(2)}) collective-permute-start(f32[58,8,256]{2,1,0:T(8,128)S(1)} %get-tuple-element.36.after), channel_id=1, source_target_pairs={{0,3},{1,0},{2,1},{3,2},{4,7},{5,4},{6,5},{7,6},{8,11},{9,8},{10,9... | collective-permute-start | bytes 1425416 | tf_op jit(solution)/shard_map/ppermute | solution.py:484
  5.5 1.3 %cut_rest.1 = (f32[54,8,256]{2,1,0:T(8,128)S(1)}, f32[54,8,256]{2,1,0:T(8,128)S(1)}) custom-call(f32[13,8,64,256]{3,2,1,0:T(8,128)} %coefs.5, f32[58,8,256]{2,1,0:T(8,128)S(1)} %get-tuple-element.36.after), custom_call_target="tpu_custom_call" | custom-call | tf_op jit(solution)/shard_map/cut_rest/pallas_call | solution.py:36
  6.8 0.2 collective-permute-start.2
  7.0 2.6 %collective-permute-start.3 = (f32[54,8,256]{2,1,0:T(8,128)S(1)}, f32[54,8,256]{2,1,0:T(8,128)S(1)}, u32[]{:S(2)}, u32[]{:S(2)}) collective-permute-start(f32[54,8,256]{2,1,0:T(8,128)S(1)} %get-tuple-element.37.after), channel_id=1, source_target_pairs={{0,3},{1,0},{2,1},{3,2},{4,7},{5,4},{6,5},{7,6},{8,11},{9,8},{10,9... | collective-permute-start | bytes 1327112 | tf_op jit(solution)/shard_map/ppermute | solution.py:484
  9.5 3.2 %load.1 = (f32[8,80,256]{2,1,0:T(8,128)S(1)}, f32[13,512,256]{2,1,0:T(8,128)S(1)}) custom-call(f32[8,64,256]{2,1,0:T(8,128)} %rhs.3, f32[13,8,64,256]{3,2,1,0:T(8,128)} %coefs.5, f32[54,8,256]{2,1,0:T(8,128)S(1)} %get-tuple-element.37.after), custom_call_target="tpu_custom_call" | custom-call | tf_op jit(solution)/shard_map/load/pallas_call | solution.py:36
  12.7 0.9 %collective-permute-done.y_below = f32[58,8,256]{2,1,0:T(8,128)S(1)} collective-permute-done((f32[58,8,256]{2,1,0:T(8,128)S(1)}, f32[58,8,256]{2,1,0:T(8,128)S(1)}, u32[]{:S(2)}, u32[]{:S(2)}) %collective-permute-start) | collective-permute-done | bytes 475168 | tf_op jit(solution)/shard_map/ppermute | solution.py:484
  13.7 1.5 %collective-permute-done.1.y_above = f32[58,8,256]{2,1,0:T(8,128)S(1)} collective-permute-done((f32[58,8,256]{2,1,0:T(8,128)S(1)}, f32[58,8,256]{2,1,0:T(8,128)S(1)}, u32[]{:S(2)}, u32[]{:S(2)}) %collective-permute-start.1) | collective-permute-done | bytes 475168 | tf_op jit(solution)/shard_map/ppermute | solution.py:484
  15.2 0.0 copy-start
  15.2 0.2 face.1
  15.3 5.3 %collective-permute-start.4 = (f32[3,80,256]{2,1,0:T(8,128)S(1)}, f32[3,80,256]{2,1,0:T(8,128)S(1)}, u32[]{:S(2)}, u32[]{:S(2)}) collective-permute-start(f32[3,80,256]{2,1,0:T(8,128)S(1)} %get-tuple-element.43.my_high), channel_id=1, source_target_pairs={{0,4},{4,8},{8,12},{12,16},{16,20},{20,24},{24,28},{28,32},{32,36}... | collective-permute-start | bytes 737288 | tf_op jit(solution)/shard_map/ppermute | solution.py:484
  20.6 0.0 collective-permute-start.5
  20.7 0.7 first_own.1
  21.4 1.8 %collective-permute-done.2.z_below = f32[54,8,256]{2,1,0:T(8,128)S(1)} collective-permute-done((f32[54,8,256]{2,1,0:T(8,128)S(1)}, f32[54,8,256]{2,1,0:T(8,128)S(1)}, u32[]{:S(2)}, u32[]{:S(2)}) %collective-permute-start.2) | collective-permute-done | bytes 442400 | tf_op jit(solution)/shard_map/ppermute | solution.py:484
  23.1 1.5 %collective-permute-done.3.z_above = f32[54,8,256]{2,1,0:T(8,128)S(1)} collective-permute-done((f32[54,8,256]{2,1,0:T(8,128)S(1)}, f32[54,8,256]{2,1,0:T(8,128)S(1)}, u32[]{:S(2)}, u32[]{:S(2)}) %collective-permute-start.3) | collective-permute-done | bytes 442400 | tf_op jit(solution)/shard_map/ppermute | solution.py:484
  24.6 0.0 copy-done
  24.6 1.7 %first_inner.1 = (f32[10,80,256]{2,1,0:T(8,128)S(1)}, f32[8,80,256]{2,1,0:T(8,128)S(1)}) custom-call(f32[4]{0:T(128)S(1)} %copy-done, f32[13,512,256]{2,1,0:T(8,128)S(1)} %get-tuple-element.38.own, f32[54,8,256]{2,1,0:T(8,128)S(1)} %collective-permute-done.2.z_below, ...), custom_call_target="tpu_custom_call", output_to_operand_aliasing={{0}: (7, {})} | custom-call | tf_op jit(solution)/shard_map/first_inner/pallas_call | solution.py:36
  26.3 0.0 collective-permute-done.4.far_low
  26.3 0.2 collective-permute-done.5.far_high
  26.5 1.0 %first_outer.1 = (f32[10,80,256]{2,1,0:T(8,128)S(1)}, f32[8,80,256]{2,1,0:T(8,128)S(1)}, f32[2,80,256]{2,1,0:T(8,128)S(1)}, f32[2,80,256]{2,1,0:T(8,128)S(1)}) custom-call(f32[4]{0:T(128)S(1)} %copy-done, f32[13,512,256]{2,1,0:T(8,128)S(1)} %get-tuple-element.38.own, ...), custom_call_target="tpu_custom_call", output_to_operand_aliasing={{0}: (11, {}), {1}: (12, {})} | custom-call | tf_op jit(solution)/shard_map/first_outer/pallas_call | solution.py:36
  27.6 3.1 %collective-permute-start.7 = (f32[2,80,256]{2,1,0:T(8,128)S(1)}, f32[2,80,256]{2,1,0:T(8,128)S(1)}, u32[]{:S(2)}, u32[]{:S(2)}) collective-permute-start(f32[2,80,256]{2,1,0:T(8,128)S(1)} %get-tuple-element.49.refs_0_), channel_id=1, source_target_pairs={{0,252},{4,0},{8,4},{12,8},{16,12},{20,16},{24,20},{28,24},{32,28}... | collective-permute-start | bytes 491528 | tf_op jit(solution)/shard_map/ppermute | solution.py:484
  30.6 0.7 collective-permute-start.6
  31.3 1.9 %inner.3 = (f32[10,80,256]{2,1,0:T(8,128)S(1)}, f32[8,80,256]{2,1,0:T(8,128)S(1)}) custom-call(f32[4]{0:T(128)S(1)} %copy-done, f32[13,512,256]{2,1,0:T(8,128)S(1)} %get-tuple-element.38.own, f32[54,8,256]{2,1,0:T(8,128)S(1)} %collective-permute-done.2.z_below, f32[54,8,256]{2,1,0:T(8,128)S(1)} %collective-permute-done.3.z_above, ...), custom_call_target="tpu_custom_call" | custom-call | tf_op jit(solution)/shard_map/inner/pallas_call | solution.py:36
  33.2 1.0 %collective-permute-done.7.refs_3_ = f32[2,80,256]{2,1,0:T(8,128)S(1)} collective-permute-done((f32[2,80,256]{2,1,0:T(8,128)S(1)}, f32[2,80,256]{2,1,0:T(8,128)S(1)}, u32[]{:S(2)}, u32[]{:S(2)}) %collective-permute-start.7) | collective-permute-done | bytes 163872 | tf_op jit(solution)/shard_map/ppermute | solution.py:484
  34.2 3.2 %collective-permute-done.6.refs_2_ = f32[2,80,256]{2,1,0:T(8,128)S(1)} collective-permute-done((f32[2,80,256]{2,1,0:T(8,128)S(1)}, f32[2,80,256]{2,1,0:T(8,128)S(1)}, u32[]{:S(2)}, u32[]{:S(2)}) %collective-permute-start.6) | collective-permute-done | bytes 163872 | tf_op jit(solution)/shard_map/ppermute | solution.py:484
  37.4 1.0 %outer.3 = (f32[10,80,256]{2,1,0:T(8,128)S(1)}, f32[8,80,256]{2,1,0:T(8,128)S(1)}, f32[2,80,256]{2,1,0:T(8,128)S(1)}, f32[2,80,256]{2,1,0:T(8,128)S(1)}) custom-call(f32[4]{0:T(128)S(1)} %copy-done, f32[13,512,256]{2,1,0:T(8,128)S(1)} %get-tuple-element.38.own, ...), custom_call_target="tpu_custom_call", output_to_operand_aliasing={{0}: (15, {}), {1}: (16, {})} | custom-call | tf_op jit(solution)/shard_map/outer/pallas_call | solution.py:36
  38.5 7.3 %collective-permute-start.9 = (f32[2,80,256]{2,1,0:T(8,128)S(1)}, f32[2,80,256]{2,1,0:T(8,128)S(1)}, u32[]{:S(2)}, u32[]{:S(2)}) collective-permute-start(f32[2,80,256]{2,1,0:T(8,128)S(1)} %get-tuple-element.54.refs_0_), channel_id=1, source_target_pairs={{0,252},{4,0},{8,4},{12,8},{16,12},{20,16},{24,20},{28,24},{32,28}... | collective-permute-start | bytes 491528 | tf_op jit(solution)/shard_map/ppermute | solution.py:484
  45.7 0.0 collective-permute-start.8
  45.7 2.0 %inner.4 = (f32[10,80,256]{2,1,0:T(8,128)S(1)}, f32[8,80,256]{2,1,0:T(8,128)S(1)}) custom-call(f32[4]{0:T(128)S(1)} %copy-done, f32[13,512,256]{2,1,0:T(8,128)S(1)} %get-tuple-element.38.own, f32[54,8,256]{2,1,0:T(8,128)S(1)} %collective-permute-done.2.z_below, f32[54,8,256]{2,1,0:T(8,128)S(1)} %collective-permute-done.3.z_above, ...), custom_call_target="tpu_custom_call" | custom-call | tf_op jit(solution)/shard_map/inner/pallas_call | solution.py:36
  47.7 0.0 collective-permute-done.9.refs_3_
  47.7 0.3 collective-permute-done.8.refs_2_
  48.0 1.0 %outer.4 = (f32[10,80,256]{2,1,0:T(8,128)S(1)}, f32[8,80,256]{2,1,0:T(8,128)S(1)}, f32[2,80,256]{2,1,0:T(8,128)S(1)}, f32[2,80,256]{2,1,0:T(8,128)S(1)}) custom-call(f32[4]{0:T(128)S(1)} %copy-done, f32[13,512,256]{2,1,0:T(8,128)S(1)} %get-tuple-element.38.own, ...), custom_call_target="tpu_custom_call", output_to_operand_aliasing={{0}: (15, {}), {1}: (16, {})} | custom-call | tf_op jit(solution)/shard_map/outer/pallas_call | solution.py:36
  49.0 6.0 %collective-permute-start.11 = (f32[2,80,256]{2,1,0:T(8,128)S(1)}, f32[2,80,256]{2,1,0:T(8,128)S(1)}, u32[]{:S(2)}, u32[]{:S(2)}) collective-permute-start(f32[2,80,256]{2,1,0:T(8,128)S(1)} %get-tuple-element.59.refs_0_), channel_id=1, source_target_pairs={{0,252},{4,0},{8,4},{12,8},{16,12},{20,16},{24,20},{28,24},{32,28}... | collective-permute-start | bytes 491528 | tf_op jit(solution)/shard_map/ppermute | solution.py:484
  55.0 0.0 collective-permute-start.10
  55.0 0.4 early_gram.1.refs_4_.early
  55.4 2.0 %inner.5 = (f32[10,80,256]{2,1,0:T(8,128)S(1)}, f32[8,80,256]{2,1,0:T(8,128)S(1)}) custom-call(f32[4]{0:T(128)S(1)} %copy-done, f32[13,512,256]{2,1,0:T(8,128)S(1)} %get-tuple-element.38.own, f32[54,8,256]{2,1,0:T(8,128)S(1)} %collective-permute-done.2.z_below, f32[54,8,256]{2,1,0:T(8,128)S(1)} %collective-permute-done.3.z_above, ...), custom_call_target="tpu_custom_call" | custom-call | tf_op jit(solution)/shard_map/inner/pallas_call | solution.py:36
  57.4 0.0 collective-permute-done.11.refs_3_
  57.4 0.0 collective-permute-done.10.refs_2_
  57.4 0.9 %outer.5 = (f32[10,80,256]{2,1,0:T(8,128)S(1)}, f32[8,80,256]{2,1,0:T(8,128)S(1)}) custom-call(f32[4]{0:T(128)S(1)} %copy-done, f32[13,512,256]{2,1,0:T(8,128)S(1)} %get-tuple-element.38.own, f32[54,8,256]{2,1,0:T(8,128)S(1)} %collective-permute-done.2.z_below, ...), custom_call_target="tpu_custom_call", output_to_operand_aliasing={{0}: (16, {}), {1}: (17, {})} | custom-call | tf_op jit(solution)/shard_map/outer/pallas_call | solution.py:36
  58.3 0.3 late_gram.1
  58.6 23.3 %all_to_all.11 = f32[256,1,128]{2,1,0:T(1,128)S(1)} all-to-all(f32[256,1,128]{2,1,0:T(1,128)S(1)} %bitcast.5), channel_id=1, replica_groups=mesh['gx_0'=4,'gx_1'=8,'gx_2'=2,'gy'=4] {'gx_0','gx_1','gx_2','gy'}, dimensions={0} | all-to-all | bytes 262144 | tf_op jit(solution)/shard_map/all_to_all | solution.py:554
  82.0 3.4 %final.1 = (f32[5,8,64,256]{3,2,1,0:T(8,128)}, f32[5,5]{1,0:T(8,128)}, f32[8,64,256]{2,1,0:T(8,128)}, f32[8,64,256]{2,1,0:T(8,128)}) custom-call(f32[4]{0:T(128)S(1)} %copy-done, f32[256,128]{1,0:T(8,128)S(1)} %bitcast.4, f32[8,80,256]{2,1,0:T(8,128)S(1)} %get-tuple-element.41.field.refs_0_.v0.refs_2_, ...), custom_call_target="tpu_custom_call" | custom-call | tf_op jit(solution)/shard_map/final/pallas_call | solution.py:36
Async XLA Ops:
  2.0 11.7 %collective-permute-start = (f32[58,8,256]{2,1,0:T(8,128)S(1)}, f32[58,8,256]{2,1,0:T(8,128)S(1)}, u32[]{:S(2)}, u32[]{:S(2)}) collective-permute-start(f32[58,8,256]{2,1,0:T(8,128)S(1)} %get-tuple-element.39), channel_id=1, source_target_pairs={{0,1},{1,2},{2,3},{3,0},{4,5},{5,6},{6,7},{7,4},{8,9},{9,10},{10,1... | collective-permute-start | bytes 1425416 | tf_op jit(solution)/shard_map/ppermute | solution.py:484
  4.1 11.1 %collective-permute-start.1 = (f32[58,8,256]{2,1,0:T(8,128)S(1)}, f32[58,8,256]{2,1,0:T(8,128)S(1)}, u32[]{:S(2)}, u32[]{:S(2)}) collective-permute-start(f32[58,8,256]{2,1,0:T(8,128)S(1)} %get-tuple-element.36.after), channel_id=1, source_target_pairs={{0,3},{1,0},{2,1},{3,2},{4,7},{5,4},{6,5},{7,6},{8,11},{9,8},{10,9... | collective-permute-start | bytes 1425416 | tf_op jit(solution)/shard_map/ppermute | solution.py:484
  6.8 16.4 %collective-permute-start.2 = (f32[54,8,256]{2,1,0:T(8,128)S(1)}, f32[54,8,256]{2,1,0:T(8,128)S(1)}, u32[]{:S(2)}, u32[]{:S(2)}) collective-permute-start(f32[54,8,256]{2,1,0:T(8,128)S(1)} %get-tuple-element.42), channel_id=1, source_target_pairs={{0,1},{1,2},{2,3},{3,0},{4,5},{5,6},{6,7},{7,4},{8,9},{9,10},{10,1... | collective-permute-start | bytes 1327112 | tf_op jit(solution)/shard_map/ppermute | solution.py:484
  7.0 17.7 %collective-permute-start.3 = (f32[54,8,256]{2,1,0:T(8,128)S(1)}, f32[54,8,256]{2,1,0:T(8,128)S(1)}, u32[]{:S(2)}, u32[]{:S(2)}) collective-permute-start(f32[54,8,256]{2,1,0:T(8,128)S(1)} %get-tuple-element.37.after), channel_id=1, source_target_pairs={{0,3},{1,0},{2,1},{3,2},{4,7},{5,4},{6,5},{7,6},{8,11},{9,8},{10,9... | collective-permute-start | bytes 1327112 | tf_op jit(solution)/shard_map/ppermute | solution.py:484
  15.2 9.5 %copy-start = (f32[4]{0:T(128)S(1)}, f32[4]{0:T(128)}, u32[]{:S(2)}) copy-start(f32[4]{0:T(128)} %refs_0_.1) | copy-start | bytes 52
  15.3 11.0 %collective-permute-start.4 = (f32[3,80,256]{2,1,0:T(8,128)S(1)}, f32[3,80,256]{2,1,0:T(8,128)S(1)}, u32[]{:S(2)}, u32[]{:S(2)}) collective-permute-start(f32[3,80,256]{2,1,0:T(8,128)S(1)} %get-tuple-element.43.my_high), channel_id=1, source_target_pairs={{0,4},{4,8},{8,12},{12,16},{16,20},{20,24},{24,28},{28,32},{32,36}... | collective-permute-start | bytes 737288 | tf_op jit(solution)/shard_map/ppermute | solution.py:484
  20.6 5.9 %collective-permute-start.5 = (f32[3,80,256]{2,1,0:T(8,128)S(1)}, f32[3,80,256]{2,1,0:T(8,128)S(1)}, u32[]{:S(2)}, u32[]{:S(2)}) collective-permute-start(f32[3,80,256]{2,1,0:T(8,128)S(1)} %get-tuple-element.44.my_low), channel_id=1, source_target_pairs={{0,252},{4,0},{8,4},{12,8},{16,12},{20,16},{24,20},{28,24},{32,28}... | collective-permute-start | bytes 737288 | tf_op jit(solution)/shard_map/ppermute | solution.py:484
  27.6 6.6 %collective-permute-start.7 = (f32[2,80,256]{2,1,0:T(8,128)S(1)}, f32[2,80,256]{2,1,0:T(8,128)S(1)}, u32[]{:S(2)}, u32[]{:S(2)}) collective-permute-start(f32[2,80,256]{2,1,0:T(8,128)S(1)} %get-tuple-element.49.refs_0_), channel_id=1, source_target_pairs={{0,252},{4,0},{8,4},{12,8},{16,12},{20,16},{24,20},{28,24},{32,28}... | collective-permute-start | bytes 491528 | tf_op jit(solution)/shard_map/ppermute | solution.py:484
  30.6 6.8 %collective-permute-start.6 = (f32[2,80,256]{2,1,0:T(8,128)S(1)}, f32[2,80,256]{2,1,0:T(8,128)S(1)}, u32[]{:S(2)}, u32[]{:S(2)}) collective-permute-start(f32[2,80,256]{2,1,0:T(8,128)S(1)} %get-tuple-element.50.refs_1_), channel_id=1, source_target_pairs={{0,4},{4,8},{8,12},{12,16},{16,20},{20,24},{24,28},{28,32},{32,36}... | collective-permute-start | bytes 491528 | tf_op jit(solution)/shard_map/ppermute | solution.py:484
  38.5 9.2 %collective-permute-start.9 = (f32[2,80,256]{2,1,0:T(8,128)S(1)}, f32[2,80,256]{2,1,0:T(8,128)S(1)}, u32[]{:S(2)}, u32[]{:S(2)}) collective-permute-start(f32[2,80,256]{2,1,0:T(8,128)S(1)} %get-tuple-element.54.refs_0_), channel_id=1, source_target_pairs={{0,252},{4,0},{8,4},{12,8},{16,12},{20,16},{24,20},{28,24},{32,28}... | collective-permute-start | bytes 491528 | tf_op jit(solution)/shard_map/ppermute | solution.py:484
  45.7 2.3 %collective-permute-start.8 = (f32[2,80,256]{2,1,0:T(8,128)S(1)}, f32[2,80,256]{2,1,0:T(8,128)S(1)}, u32[]{:S(2)}, u32[]{:S(2)}) collective-permute-start(f32[2,80,256]{2,1,0:T(8,128)S(1)} %get-tuple-element.55.refs_1_), channel_id=1, source_target_pairs={{0,4},{4,8},{8,12},{12,16},{16,20},{20,24},{24,28},{28,32},{32,36}... | collective-permute-start | bytes 491528 | tf_op jit(solution)/shard_map/ppermute | solution.py:484
  49.0 8.4 %collective-permute-start.11 = (f32[2,80,256]{2,1,0:T(8,128)S(1)}, f32[2,80,256]{2,1,0:T(8,128)S(1)}, u32[]{:S(2)}, u32[]{:S(2)}) collective-permute-start(f32[2,80,256]{2,1,0:T(8,128)S(1)} %get-tuple-element.59.refs_0_), channel_id=1, source_target_pairs={{0,252},{4,0},{8,4},{12,8},{16,12},{20,16},{24,20},{28,24},{32,28}... | collective-permute-start | bytes 491528 | tf_op jit(solution)/shard_map/ppermute | solution.py:484
  55.0 2.4 %collective-permute-start.10 = (f32[2,80,256]{2,1,0:T(8,128)S(1)}, f32[2,80,256]{2,1,0:T(8,128)S(1)}, u32[]{:S(2)}, u32[]{:S(2)}) collective-permute-start(f32[2,80,256]{2,1,0:T(8,128)S(1)} %get-tuple-element.60.refs_1_), channel_id=1, source_target_pairs={{0,4},{4,8},{8,12},{12,16},{16,20},{20,24},{24,28},{28,32},{32,36}... | collective-permute-start | bytes 491528 | tf_op jit(solution)/shard_map/ppermute | solution.py:484
